TPU v7x, 32 devices: a whole 2x2x4 slice. The times are simulated.
32 devices in a mesh: seq: 8 (over y, x, core), mp: 4 (over z).
Axes of the slice: x: 2, y: 2, z: 4, core: 2. Of those that a mesh axis runs over, the one named last changes fastest.
Arguments:
- tokens: bfloat16 [16384, 768], P('seq'), may hold values from -6 to 6
- cotangent: bfloat16 [16384, 768], P('seq'), may hold values from -6 to 6
- past_state: bfloat16 [16, 512, 768], P('seq', None, 'mp'), may hold values from -6 to 6
- positions: int32 [16, 128], P('seq'), may hold values from 0 to 511, as said below
- counts: int32 [16], P('seq'), may hold values from 16 to 128, as said below
- ln1_gain: bfloat16 [768], P('seq'), may hold values from 0.5 to 1.5
- ln1_bias: bfloat16 [768], P('seq'), may hold values from -1 to 1
- w_qkv: bfloat16 [3, 768, 768], P(None, 'seq', 'mp'), may hold values from -0.21875 to 0.21875
- b_qv: bfloat16 [2, 12, 64], P(None, 'mp', 'seq'), may hold values from -1.5 to 1.5
- w_out: bfloat16 [768, 768], P('mp', 'seq'), may hold values from -3 to 3
- b_out: bfloat16 [768], P('seq'), may hold values from -1.5 to 1.5
- ln2_gain: bfloat16 [768], P('seq'), may hold values from 0.5 to 1.5
- ln2_bias: bfloat16 [768], P('seq'), may hold values from -1 to 1
- w_up: bfloat16 [768, 3072], P('seq', 'mp'), may hold values from -0.25 to 0.25
- b_up: bfloat16 [48, 64], P('mp', 'seq'), may hold values from -2.5 to 2.5
- w_down: bfloat16 [3072, 768], P('mp', 'seq'), may hold values from -0.109375 to 0.109375
- b_down: bfloat16 [768], P('seq'), may hold values from -1.5 to 1.5
Outputs:
- out: bfloat16 [16384, 768], P('seq')
- tokens_grad: bfloat16 [16384, 768], P('seq')
- past_grad: float32 [16, 512, 768], P('seq', None, 'mp')
- ln1_gain_grad: float32 [768], P('seq')
- ln1_bias_grad: float32 [768], P('seq')
- w_qkv_grad: float32 [3, 768, 768], P(None, 'seq', 'mp')
- b_qv_grad: float32 [2, 12, 64], P(None, 'mp', 'seq')
- w_out_grad: float32 [768, 768], P('mp', 'seq')
- b_out_grad: float32 [768], P('seq')
- ln2_gain_grad: float32 [768], P('seq')
- ln2_bias_grad: float32 [768], P('seq')
- w_up_grad: float32 [768, 3072], P('seq', 'mp')
- b_up_grad: float32 [48, 64], P('mp', 'seq')
- w_down_grad: float32 [3072, 768], P('mp', 'seq')
- b_down_grad: float32 [768], P('seq')
Inputs may be any that keep to these rules, and one draw needn't show every extreme that they name: The 128 positions of one old segment are distinct. Slots 0 to counts[i] - 1 of old segment i are used; some old segment uses all 128.
All inputs are finite; a program needn't handle non-finite values.
Results may differ from a plain program's by a relative error of at most 0.03.
Values may be sent and summed in bfloat16 or wider, within the bound.
A program may use at most 192 MiB of HBM per device.

v0:
```python
import functools
import math

import jax
import jax.numpy as jnp
from jax import lax
from jax.experimental import pallas as pl
from jax.experimental.pallas import tpu as pltpu
from jax.sharding import PartitionSpec as P

NB = 256
PIVOTS = 32
NORM_EPSILON = 1e-05
RIDGE_WEIGHT = 1.0
NARROW_WIDTH = 0.01
BROAD_WIDTH = 0.05
GELU_SCALE = 0.7978845608028654
GELU_CUBIC = 0.044715

BF = jnp.bfloat16
F32 = jnp.float32
HIGHEST = lax.Precision.HIGHEST
BIG_VMEM = 60 * 1024 * 1024
MAX_VMEM = 67043328


def dot(a, b):
    return jnp.dot(a, b, preferred_element_type=F32)


def dot_nt(a, b):
    return lax.dot_general(a, b, (((1,), (1,)), ((), ())), preferred_element_type=F32)


def dot_tn(a, b, precision=None):
    return lax.dot_general(
        a, b, (((0,), (0,)), ((), ())), preferred_element_type=F32, precision=precision
    )


def norm_parts(values):
    centered = values - jnp.mean(values, axis=-1, keepdims=True)
    inverse = lax.rsqrt(jnp.mean(centered * centered, axis=-1, keepdims=True) + NORM_EPSILON)
    return centered * inverse, inverse


def norm_back(upstream, normed, inverse, gain):
    scaled = upstream * gain
    inner = scaled - jnp.mean(scaled, axis=-1, keepdims=True)
    inner = inner - normed * jnp.mean(scaled * normed, axis=-1, keepdims=True)
    return inner * inverse


def col_sum(values):
    return jnp.sum(values, axis=0, keepdims=True)


def basis_of(places, used):
    column = lax.broadcasted_iota(jnp.int32, (places.shape[0], NB), 1)
    centers = (column.astype(F32) + 0.5) / NB
    widths = jnp.where(column % 2 == 0, NARROW_WIDTH, BROAD_WIDTH).astype(F32)
    scaled = (places - centers) / widths
    return jnp.exp(-0.5 * (scaled * scaled)) * used


def meta_rows(positions, counts_ref, first, total, seg_len):
    items, slots = positions.shape
    slot = lax.broadcasted_iota(jnp.int32, (1, slots), 1)
    places, used, spots = [], [], []
    for i in range(items):
        spot = positions[i : i + 1, :].astype(F32)
        item = (first + i).astype(F32)
        places.append((item + (spot + 0.5) / seg_len) / total)
        used.append((slot < counts_ref[i]).astype(F32))
        spots.append(spot)
    return jnp.concatenate(
        places + used + spots + [jnp.zeros((8 - 3 * items, slots), F32)], axis=0
    )


def iotas(shape):
    return lax.broadcasted_iota(jnp.int32, shape, 0), lax.broadcasted_iota(jnp.int32, shape, 1)


def small_rows(stack, b_qv, b_up_t, s, width, head):
    part, piece = stack.shape[1], b_up_t.shape[0]
    row, lane = iotas((part, width))
    rows = [jnp.dot(stack, (lane == s * part + row).astype(F32), preferred_element_type=F32)]
    row, lane = iotas((piece, width))
    repeat = (lax.rem(lane, piece) == row).astype(F32)
    _, lane = iotas((1, width))
    half = width // 2
    bias = jnp.zeros((1, width), F32)
    for h in range(b_qv.shape[0]):
        spread = jnp.dot(b_qv[h], repeat, preferred_element_type=F32)
        for t in range(2):
            at = h * head + t * half + s * piece
            bias = bias + jnp.where((lane >= at) & (lane < at + piece), spread[t : t + 1], 0.0)
    row, lane = iotas((b_up_t.shape[1], width))
    spread = jnp.dot(b_up_t, (lane // head == row).astype(F32), preferred_element_type=F32)
    row, lane = iotas((piece, width))
    up = jnp.sum(jnp.where(lax.rem(lane, head) == s * piece + row, spread, 0.0), axis=0, keepdims=True)
    return jnp.concatenate(rows + [bias, up, jnp.zeros((8, width), F32)], axis=0).astype(BF)


def small_pieces(own, s, part, piece, head, heads):
    width = own.shape[1]
    half = width // 2
    row, lane = iotas((width, part + 2 * heads * piece))
    slot = lane - part
    spot = (slot // (2 * piece)) * head + (lax.rem(slot, 2 * piece) // piece) * half
    source = jnp.where(lane < part, s * part + lane, spot + s * piece + lax.rem(slot, piece))
    picked = jnp.dot(
        own, (row == source).astype(F32), preferred_element_type=F32, precision=HIGHEST
    )
    at = [part + i * piece for i in range(2 * heads)]
    flat = [picked[6:7, i : i + piece] for i in at]
    biases = [jnp.concatenate(flat[2 * h : 2 * h + 2], axis=0) for h in range(heads)]
    row, lane = iotas((piece, width))
    masked = jnp.where(lax.rem(lane, head) == s * piece + row, own[7:8], 0.0)
    row, lane = iotas((width, width // head))
    up = jnp.dot(
        masked, (row // head == lane).astype(F32), preferred_element_type=F32, precision=HIGHEST
    )
    return picked[:, :part], biases, up


def position_of(column, i, items):
    return column[:, 2 * items + i : 2 * items + i + 1].astype(jnp.int32)


def inverse_2(a, b, c, d):
    scale = 1.0 / (a * d - b * c)
    return d * scale, -(b * scale), -(c * scale), a * scale


def product_2(x, y):
    return (
        x[0] * y[0] + x[1] * y[2],
        x[0] * y[1] + x[1] * y[3],
        x[2] * y[0] + x[3] * y[2],
        x[2] * y[1] + x[3] * y[3],
    )


def invert_step(mat_ref):
    block = PIVOTS
    lane = lax.broadcasted_iota(jnp.int32, (block, NB), 1)
    line = lax.broadcasted_iota(jnp.int32, (block, NB), 0)
    panel = mat_ref[0:block, :]
    for k in range(0, block, 4):
        cols = [jnp.broadcast_to(panel[:, k + j : k + j + 1], panel.shape) for j in range(4)]
        at = [[cols[j][k + i : k + i + 1] for j in range(4)] for i in range(4)]
        head = inverse_2(at[0][0], at[0][1], at[1][0], at[1][1])
        upper = (at[0][2], at[0][3], at[1][2], at[1][3])
        lower = (at[2][0], at[2][1], at[3][0], at[3][1])
        right, left = product_2(head, upper), product_2(lower, head)
        minus = product_2(lower, right)
        tail = inverse_2(
            at[2][2] - minus[0], at[2][3] - minus[1], at[3][2] - minus[2], at[3][3] - minus[3]
        )
        rt, tl = product_2(right, tail), product_2(tail, left)
        back = product_2(rt, left)
        inverse = (
            (head[0] + back[0], head[1] + back[1], -rt[0], -rt[1]),
            (head[2] + back[2], head[3] + back[3], -rt[2], -rt[3]),
            (-tl[0], -tl[1], tail[0], tail[1]),
            (-tl[2], -tl[3], tail[2], tail[3]),
        )
        inside = (lane >= k) & (lane < k + 4)
        rows = [
            jnp.where(inside[0:1], (lane[0:1] == k + j).astype(F32), panel[k + j : k + j + 1])
            for j in range(4)
        ]
        new = [
            (m[0] * rows[0] + m[1] * rows[1]) + (m[2] * rows[2] + m[3] * rows[3]) for m in inverse
        ]
        rest = jnp.where(inside, 0.0, panel) - (
            (cols[0] * new[0] + cols[1] * new[1]) + (cols[2] * new[2] + cols[3] * new[3])
        )
        for i in range(4):
            rest = jnp.where(line == k + i, new[i], rest)
        panel = rest
    mat_ref[0:block, :] = panel
    row = lax.broadcasted_iota(jnp.int32, (NB, NB), 0)
    col = lax.broadcasted_iota(jnp.int32, (NB, NB), 1)
    mat = mat_ref[...]
    inside_row = row < block
    inside_col = col < block
    left = jnp.where(inside_col & ~inside_row, mat, 0.0)
    right = jnp.where(inside_row, mat, 0.0)
    update = jnp.dot(left, right, preferred_element_type=F32, precision=HIGHEST)
    mat = jnp.where(inside_row, mat, jnp.where(inside_col, 0.0, mat) - update)
    mat = pltpu.roll(mat, NB - block, 1)
    mat_ref[0 : NB - block, :] = mat[block:, :]
    mat_ref[NB - block :, :] = mat[:block, :]


def owner_basis(meta, items):
    column = meta.T
    rows = [
        basis_of(column[:, i : i + 1], column[:, items + i : items + i + 1]) for i in range(items)
    ]
    return jnp.concatenate(rows, axis=0)


def clear_moments(mat_ref, mom_ref):
    row = lax.broadcasted_iota(jnp.int32, (NB, NB), 0)
    col = lax.broadcasted_iota(jnp.int32, (NB, NB), 1)
    mat_ref[...] = jnp.where(row == col, RIDGE_WEIGHT, 0.0)
    mom_ref[...] = jnp.zeros_like(mom_ref)


def coefficients(mat_ref, mom_ref):
    return jnp.dot(mat_ref[...], mom_ref[...], preferred_element_type=F32, precision=HIGHEST)


def pick_samples(past, meta, items):
    slots, seg_len = meta.shape[1], past.shape[2]
    column = meta.T
    at = lax.broadcasted_iota(jnp.int32, (slots, seg_len), 1)
    rows = []
    for i in range(items):
        pick = (at == position_of(column, i, items)).astype(F32).astype(BF)
        rows.append(dot_nt(pick, past[i]).astype(BF))
    return jnp.concatenate(rows, axis=0)


def sample_kernel(past_ref, meta_ref, out_ref, *, items):
    out_ref[...] = pick_samples(past_ref[...], meta_ref[...], items)


def sample_rows(past, meta):
    items, width, seg_len = past.shape
    return pl.pallas_call(
        functools.partial(sample_kernel, items=items),
        out_shape=jax.ShapeDtypeStruct((items * meta.shape[1], width), BF),
        name="sample_rows",
    )(past, meta)


def solve_kernel(sampled_ref, meta_ref, coef_ref, inv_ref, mat_ref, mom_ref, *, items):
    clear_moments(mat_ref, mom_ref)

    def owner(s, carry):
        rows = owner_basis(meta_ref[s], items)
        mat_ref[...] += dot_tn(rows, rows, HIGHEST)
        mom_ref[...] += dot_tn(rows, sampled_ref[s].astype(F32), HIGHEST)
        return carry

    lax.fori_loop(0, meta_ref.shape[0], owner, 0)

    def step(s, carry):
        invert_step(mat_ref)
        return carry

    lax.fori_loop(0, NB // PIVOTS, step, 0)
    inv_ref[...] = mat_ref[...]
    coef_ref[...] = coefficients(mat_ref, mom_ref).astype(BF)


def solve_memory(sampled, meta, items):
    width = sampled.shape[-1]
    return pl.pallas_call(
        functools.partial(solve_kernel, items=items),
        out_shape=(
            jax.ShapeDtypeStruct((NB, width), BF),
            jax.ShapeDtypeStruct((NB, NB), F32),
        ),
        scratch_shapes=[pltpu.VMEM((NB, NB), F32), pltpu.VMEM((NB, width), F32)],
        compiler_params=pltpu.CompilerParams(vmem_limit_bytes=BIG_VMEM),
        name="solve_memory",
    )(sampled, meta)


def give_past(gmem, coef_ref, vec_ref, inv_ref, meta_ref, out_ref, gv_ref):
    slots = meta_ref.shape[1]
    item_count, width, seg_len = out_ref.shape
    normed, inverse = norm_parts(coef_ref[...].astype(F32))
    coef_grad = norm_back(gmem, normed, inverse, vec_ref[0, 0:1, :])
    gv_ref[...] = jnp.zeros_like(gv_ref)
    gv_ref[0:1, :] = col_sum(gmem * normed)
    gv_ref[1:2, :] = col_sum(gmem)
    part = lax.axis_index("mp")
    mine = jnp.zeros((coef_grad.shape[0], width), F32)
    for m in range(coef_grad.shape[1] // width):
        mine = jnp.where(part == m, coef_grad[:, m * width : (m + 1) * width], mine)
    moment = jnp.dot(inv_ref[...], mine, preferred_element_type=F32, precision=HIGHEST)
    at = lax.broadcasted_iota(jnp.int32, (slots, seg_len), 1)
    column = meta_ref[...].T
    for i in range(item_count):
        rows = basis_of(column[:, i : i + 1], column[:, item_count + i : item_count + i + 1])
        sampled = jnp.dot(rows, moment, preferred_element_type=F32, precision=HIGHEST)
        spread = (at == position_of(column, i, item_count)).astype(F32)
        out_ref[i] = dot_tn(sampled, spread, HIGHEST)


def past_kernel(gmem_ref, coef_ref, vec_ref, inv_ref, meta_ref, out_ref, gv_ref):
    give_past(gmem_ref[...], coef_ref, vec_ref, inv_ref, meta_ref, out_ref, gv_ref)


def past_grads(gmem, coef, vec, inv, meta, items, seg_len, width):
    return pl.pallas_call(
        past_kernel,
        out_shape=(
            jax.ShapeDtypeStruct((items, width, seg_len), F32),
            jax.ShapeDtypeStruct((8, coef.shape[1]), F32),
        ),
        compiler_params=pltpu.CompilerParams(vmem_limit_bytes=BIG_VMEM),
        name="past_grads",
    )(gmem, coef, vec, inv, meta)


MESH = pl.DeviceIdType.MESH
LINE = 4
PLANE = 8
NEAR = (0, -1, 1, -2, 2, -3, 3)


class Place:
    def __init__(self):
        self.s = lax.axis_index("seq")
        self.z = lax.axis_index("mp")
        core = lax.rem(self.s, 2)
        x = lax.rem(self.s // 2, 2)
        y = self.s // 4
        self.turn = 1 - 2 * core
        self.partner = self.s + self.turn
        self.sx = self.s + 2 - 4 * x
        self.sy = self.s + 4 - 8 * y
        self.sd = self.sx + 4 - 8 * y
        self.low = self.z > 0
        self.high = self.z < LINE - 1
        self.near = [
            (
                d,
                valid(self.z + d),
                self.z + d,
                lax.rem(self.z + d + LINE, 2) == 1,
                lax.rem(self.z + d + LINE, 2) == 0,
            )
            for d in NEAR
        ]


def valid(m):
    return (m >= 0) & (m < LINE)


def when(conditions, act):
    conditions = [c for c in conditions if c is not None]
    if conditions:
        pl.when(functools.reduce(lambda a, b: a & b, conditions))(act)
    else:
        act()


def greet(place, whole_line=False):
    barrier = pltpu.get_barrier_semaphore()

    def signal(seq, z):
        pl.semaphore_signal(barrier, inc=1, device_id=(seq, z), device_id_type=MESH)

    for seq in (place.partner, place.sx, place.sy):
        signal(seq, place.z)
    for d, ok, m, odd, even in place.near[1:]:
        if whole_line or abs(d) == 1:
            when((ok,), lambda: signal(place.s, m))
    if whole_line:
        peers = LINE - 1
    else:
        peers = (place.z + LINE - 1) // LINE + (2 * LINE - 2 - place.z) // LINE
    pl.semaphore_wait(barrier, 3 + peers)


UP, DOWN, ACROSS_X, ACROSS_Y, PARTNER = range(5)


class Spread:
    def __init__(self, place, src, dst, send, recv, local, line=True):
        self.p, self.src, self.dst = place, src, dst
        self.send, self.recv, self.line = send, recv, line
        self.rows = src.shape[0]
        self.sent = []
        self.mine = place.z if line else 0
        self.around = place.near if line else [(0, None, 0, None, None)]
        self.own = pltpu.make_async_copy(src, self.at(self.mine, place.s), local)

    def at(self, m, s):
        return self.dst.at[m, pl.ds(s * self.rows, self.rows), :]

    def copy(self, direction, m, s, own=False):
        p = self.p
        device = (
            (p.s, p.z + 1),
            (p.s, p.z - 1),
            (p.sx, p.z),
            (p.sy, p.z),
            (p.partner, p.z),
        )[direction]
        return pltpu.make_async_remote_copy(
            src_ref=self.src if own else self.at(m, s),
            dst_ref=self.at(m, s),
            send_sem=self.send.at[direction, m * 4 + s // 2],
            recv_sem=self.recv.at[m * PLANE + s],
            device_id=device,
            device_id_type=MESH,
        )

    def start(self, conditions, *what, **how):
        when(conditions, lambda: self.copy(*what, **how).start())
        self.sent.append((conditions, what, how))

    def arrived(self, m, s):
        self.copy(PARTNER, m, s).wait_recv()

    def first(self):
        p, m = self.p, self.mine
        self.own.start()
        if self.line:
            self.start((p.high,), UP, m, p.s, own=True)
            self.start((p.low,), DOWN, m, p.s, own=True)
        for direction in (ACROSS_X, ACROSS_Y, PARTNER):
            self.start((), direction, m, p.s, own=True)

    def along(self, d, ok, m, odd, even):
        p = self.p
        when((ok,), lambda: self.arrived(m, p.s))
        if d < 0:
            self.start((ok, p.high), UP, m, p.s)
        else:
            self.start((ok, p.low), DOWN, m, p.s)
        for direction in (ACROSS_X, ACROSS_Y, PARTNER):
            self.start((ok,), direction, m, p.s)

    def across(self, d, ok, m, odd, even):
        p = self.p
        when((ok,), lambda: self.arrived(m, p.sx))
        if self.line:
            self.start((ok, odd), ACROSS_Y, m, p.sx)
        self.start((ok,), PARTNER, m, p.sx)
        when((ok,), lambda: self.arrived(m, p.sy))
        if self.line:
            self.start((ok, even), ACROSS_X, m, p.sy)
        else:
            self.start((), ACROSS_X, m, p.sy)
        self.start((ok,), PARTNER, m, p.sy)

    def corner(self, d, ok, m, odd, even):
        p = self.p
        when((ok,), lambda: self.arrived(m, p.sd))
        self.start((ok,), PARTNER, m, p.sd)

    def part(self, kind, d):
        if kind == 0:
            return self.first
        act = (self.along, self.across, self.corner)[kind - 1]
        return functools.partial(act, *self.around[NEAR.index(d)])

    def steps(self, kind):
        return [self.part(kind, d) for d in NEAR if d or kind > 1]

    def close(self, m):
        p = self.p
        for s in (p.s, p.sx, p.sy, p.sd):
            self.arrived(m, s + p.turn)

    def settle(self):
        for conditions, what, how in self.sent:
            when(conditions, lambda: self.copy(*what, **how).wait_send())


class DirectSpread(Spread):
    def throw(self, m):
        p = self.p
        return pltpu.make_async_remote_copy(
            src_ref=self.src,
            dst_ref=self.at(self.mine, p.s),
            send_sem=self.send.at[UP, m],
            recv_sem=self.recv.at[self.mine * PLANE + p.s],
            device_id=(p.s, m),
            device_id_type=MESH,
        )

    def first(self):
        p, m = self.p, self.mine
        self.own.start()
        for d, ok, to, odd, even in self.around[1:]:
            when((ok,), lambda: self.throw(to).start())
        for direction in (ACROSS_X, ACROSS_Y, PARTNER):
            self.start((), direction, m, p.s, own=True)

    def along(self, d, ok, m, odd, even):
        when((ok,), lambda: self.arrived(m, self.p.s))
        for direction in (ACROSS_X, ACROSS_Y, PARTNER):
            self.start((ok,), direction, m, self.p.s)

    def settle(self):
        super().settle()
        for d, ok, m, odd, even in self.around[1:]:
            when((ok,), lambda: self.throw(m).wait_send())


class Line:
    def __init__(self, place, src, dst, send, recv, local):
        self.p, self.src, self.dst = place, src, dst
        self.send, self.recv = send, recv
        self.sent = []
        self.own = pltpu.make_async_copy(src, dst.at[place.z], local)

    def copy(self, up, m, own=False):
        p = self.p
        return pltpu.make_async_remote_copy(
            src_ref=self.src if own else self.dst.at[m],
            dst_ref=self.dst.at[m],
            send_sem=self.send.at[1 if up else 0, m],
            recv_sem=self.recv.at[m],
            device_id=(p.s, p.z + 1 if up else p.z - 1),
            device_id_type=MESH,
        )

    def start(self, conditions, *what, **how):
        when(conditions, lambda: self.copy(*what, **how).start())
        self.sent.append((conditions, what, how))

    def first(self):
        p = self.p
        self.own.start()
        self.start((p.high,), True, p.z, own=True)
        self.start((p.low,), False, p.z, own=True)

    def step(self, distance):
        p = self.p
        for d, ok, m, odd, even in p.near:
            if abs(d) != distance:
                continue
            when((ok,), lambda: self.copy(True, m).wait_recv())
            if d < 0:
                self.start((ok, p.high), True, m)
            else:
                self.start((ok, p.low), False, m)

    def finish_sends(self):
        for conditions, what, how in self.sent:
            when(conditions, lambda: self.copy(*what, **how).wait_send())

    def finish(self):
        self.finish_sends()
        self.own.wait()


class Collect:
    OWN, SIDE_X, SIDE_Y, CORNER = range(4)

    def __init__(self, place, grads, out, buffers, sems):
        self.p, self.grads, self.out = place, grads, out
        self.pin, self.din, self.xin, self.yin, self.zin = buffers
        self.block_sems, self.sems = sems
        self.rows = out.shape[1]
        self.columns = (place.s, place.sx, place.sy, place.sd)

    def plane(self, i):
        return i

    def unit(self, c, m, turn=0):
        s = self.columns[c] + turn
        return self.grads.at[m, :, pl.ds(s * self.rows, self.rows), :]

    def remote(self, src, dst, send, recv, device):
        return pltpu.make_async_remote_copy(
            src_ref=src,
            dst_ref=dst,
            send_sem=send,
            recv_sem=recv,
            device_id=device,
            device_id_type=MESH,
        )

    def swap(self, c, m):
        p = self.p
        return self.remote(
            self.unit(c, m, p.turn),
            self.pin.at[c, m],
            self.block_sems.at[0, c, m],
            self.block_sems.at[1, c, m],
            (p.partner, p.z),
        )

    def hop(self, kind, m, by_x=True):
        p = self.p
        src, dst, device = (
            (self.CORNER, self.din, (p.sx if by_x else p.sy, p.z)),
            (self.SIDE_X, self.xin, (p.sx, p.z)),
            (self.SIDE_Y, self.yin, (p.sy, p.z)),
        )[kind]
        return self.remote(
            self.unit(src, m),
            dst.at[m],
            self.sems.at[kind, m],
            self.sems.at[4 + kind, m],
            device,
        )

    def slot(self, m, z):
        ends = 1 // (1 + z - m)
        return m + (LINE - m) * ends

    def climb(self, m, up):
        p = self.p
        return self.remote(
            self.unit(self.OWN, m),
            self.zin.at[m if up else self.slot(m, p.z - 1)],
            self.sems.at[3, m],
            self.sems.at[7 if up else 8, m],
            (p.s, p.z + 1 if up else p.z - 1),
        )

    def climbed(self, m, up):
        zin = self.zin.at[m if up else self.slot(m, self.p.z)]
        return self.remote(
            zin, zin, self.sems.at[3, m], self.sems.at[7 if up else 8, m], (self.p.partner, self.p.z)
        )

    def add(self, c, m, *others):
        size = min(32, self.rows)
        pieces = self.rows // size

        @pl.loop(0, self.grads.shape[1] * pieces)
        def _(j):
            l = j // pieces
            at = lax.rem(j, pieces) * size
            here = pl.ds(pl.multiple_of(self.columns[c] * self.rows + at, 16), size)
            there = pl.ds(pl.multiple_of(at, 16), size)
            total = self.grads[m, l, here, :].astype(F32)
            for other in others:
                total = total + other[m, l, there, :].astype(F32)
            self.grads[m, l, here, :] = total.astype(self.grads.dtype)

    def begin(self, m):
        for c in (self.CORNER, self.SIDE_X, self.SIDE_Y, self.OWN):
            self.swap(c, m).start()

    def join(self, c, m):
        self.swap(c, m).wait_recv()
        self.add(c, m, self.pin.at[c])

    def corner(self, i):
        m = self.plane(i)
        self.join(self.CORNER, m)
        even = lax.rem(m, 2) == 0
        pl.when(even)(lambda: self.hop(0, m, True).start())
        pl.when(~even)(lambda: self.hop(0, m, False).start())

    def sides(self, i):
        m = self.plane(i)
        even = lax.rem(m, 2) == 0
        self.join(self.SIDE_X, m)
        self.join(self.SIDE_Y, m)
        pl.when(even)(lambda: self.hop(1, m).start())
        pl.when(~even)(lambda: self.hop(2, m).start())

    def relay(self, i):
        m = self.plane(i)
        even = lax.rem(m, 2) == 0
        self.hop(0, m).wait_recv()

        @pl.when(even)
        def _():
            self.add(self.SIDE_Y, m, self.din)
            self.hop(2, m).start()

        @pl.when(~even)
        def _():
            self.add(self.SIDE_X, m, self.din)
            self.hop(1, m).start()

    def line(self, i):
        p = self.p
        m = self.plane(i)
        self.join(self.OWN, m)
        self.hop(1, m).wait_recv()
        self.hop(2, m).wait_recv()
        self.add(self.OWN, m, self.xin, self.yin)

        @pl.when(m > p.z)
        def _():
            @pl.when(p.low)
            def _():
                self.climbed(m, True).wait_recv()
                self.add(self.OWN, m, self.zin)

            self.climb(m, True).start()

        @pl.when(m < p.z)
        def _():
            @pl.when(p.high)
            def _():
                self.climbed(m, False).wait_recv()
                self.add(self.OWN, m, self.zin)

            self.climb(m, False).start()

    def result(self):
        p = self.p
        self.out[...] = self.unit(self.OWN, p.z)[...].astype(F32)

        @pl.when(p.low)
        def _():
            self.climbed(p.z, True).wait_recv()
            self.out[...] += self.zin[p.z].astype(F32)

        @pl.when(p.high)
        def _():
            self.climbed(p.z, False).wait_recv()
            self.out[...] += self.zin[LINE].astype(F32)

    def part(self, kind, i):
        if kind == 4:
            return self.result
        return functools.partial((self.corner, self.sides, self.relay, self.line)[kind], i)

    def settle(self):
        @pl.loop(0, LINE)
        def _(m):
            for c in range(4):
                self.swap(c, m).wait_send()
            for kind in range(3):
                self.hop(kind, m).wait_send()
            pl.when(m != self.p.z)(lambda: self.climb(m, True).wait_send())


class DirectCollect(Collect):
    def throw(self, m):
        p = self.p
        return self.remote(
            self.unit(self.OWN, m),
            self.zin.at[p.z],
            self.sems.at[3, m],
            self.sems.at[7, p.z],
            (p.s, m),
        )

    def line(self, i):
        m = self.plane(i)
        self.join(self.OWN, m)
        self.hop(1, m).wait_recv()
        self.hop(2, m).wait_recv()
        self.add(self.OWN, m, self.xin, self.yin)
        pl.when(m != self.p.z)(lambda: self.throw(m).start())

    def result(self):
        p = self.p
        self.out[...] = self.unit(self.OWN, p.z)[...].astype(F32)
        for m in range(LINE):

            @pl.when(m != p.z)
            def _():
                zin = self.zin.at[m]
                self.remote(
                    zin, zin, self.sems.at[3, m], self.sems.at[7, m], (p.partner, p.z)
                ).wait_recv()
                self.out[...] += self.zin[m].astype(F32)


BUFFERS = ((4, LINE), (LINE,), (LINE,), (LINE,), (LINE + 1,))


def project(rows, weights, bias, local):
    return (dot(rows, weights[:, : 3 * local]) + bias[:, : 3 * local]).astype(BF)


def attend(query, keys, values, head, store, between):
    rows, local = query.shape
    half = rows // 2
    query_t = query.T * BF(1.0 / math.sqrt(head))
    value_t = values.T
    line = lax.broadcasted_iota(jnp.int32, (local, rows), 0)
    heads = []
    for h in range(local // head):
        own = (line >= h * head) & (line < (h + 1) * head)
        masked = jnp.where(own, query_t, BF(0.0))
        value_h = value_t[h * head : (h + 1) * head, :]
        parts = []
        for b in range(2):
            span = NB + (b + 1) * half
            scores = dot(keys[:span, :], masked[:, b * half : (b + 1) * half])
            key_at = lax.broadcasted_iota(jnp.int32, (half, half), 0)
            row_at = lax.broadcasted_iota(jnp.int32, (half, half), 1)
            edge = jnp.where(key_at <= row_at, scores[span - half :, :], -1e30)
            scores = jnp.concatenate([scores[: span - half, :], edge], axis=0)
            scores = jnp.exp(scores - jnp.max(scores, axis=0, keepdims=True))
            probs = (scores * (1.0 / jnp.sum(scores, axis=0, keepdims=True))).astype(BF)
            store(h, slice(0, span), slice(b * half, (b + 1) * half), probs)
            parts.append(dot(value_h[:, :span], probs))
        heads.append(jnp.concatenate(parts, axis=1).astype(BF))
        between(h)
    return jnp.concatenate(heads, axis=0)


def gelu_parts(pre):
    square = pre * pre
    inner = jnp.tanh(GELU_SCALE * (pre + GELU_CUBIC * pre * square))
    half_up = 0.5 * (1.0 + inner)
    slope = GELU_SCALE * (1.0 + 3.0 * GELU_CUBIC * square)
    return (pre * half_up).astype(BF), half_up + 0.5 * pre * (1.0 - inner * inner) * slope


def forward_kernel(
    tokens_ref,
    past_ref,
    pos_ref,
    counts_ref,
    stack_ref,
    b_qv_ref,
    b_up_ref,
    w_qkv_ref,
    w_out_ref,
    up_ref,
    down_ref,
    wa_ref,
    wu_ref,
    wd_ref,
    out_ref,
    res_ref,
    hmt_ref,
    h2t_ref,
    prob_ref,
    key_ref,
    val_ref,
    query_ref,
    att_ref,
    act_ref,
    slope_ref,
    vec_ref,
    inv_ref,
    coef_ref,
    meta_ref,
    hm_ref,
    h2_ref,
    room_ref,
    attn_ref,
    tok_ref,
    acc_ref,
    mom_ref,
    sampled_ref,
    all_sampled_ref,
    basis_ref,
    all_meta_ref,
    all_room_ref,
    coef_part_ref,
    all_coef_ref,
    wide_ref,
    past_vmem,
    flat_send,
    flat_recv,
    flat_local,
    send,
    recv,
    own_sem,
    line_send,
    line_recv,
    line_own,
    load_sem,
    *,
    items,
    head,
):
    step = pl.program_id(0)
    rows, width = tok_ref.shape
    local = query_ref.shape[2]
    place = Place()
    flat = [
        Spread(
            place, src, dst, flat_send.at[i], flat_recv.at[i], flat_local.at[i], line=False
        )
        for i, (src, dst) in enumerate(
            ((meta_ref, all_meta_ref), (sampled_ref, all_sampled_ref))
        )
    ]
    wide = [
        Spread(place, src, dst, send.at[i], recv.at[i], own_sem.at[i])
        for i, (src, dst) in enumerate(
            ((room_ref, all_room_ref), (attn_ref, wa_ref), (up_ref, wu_ref), (down_ref, wd_ref))
        )
    ]
    room, attn, up, down = wide
    line = Line(place, coef_part_ref, all_coef_ref, line_send, line_recv, line_own)

    attn_at = SOLVE_STEPS
    mlp_at = attn_at + LINE
    last = mlp_at + LINE - 1
    plan = {
        slot: [wide[i].part(kind, d) for i, kind, d in steps] for slot, steps in FORWARD_PLAN
    }

    def transfers(at, position):
        if plan.get((at, position)):

            @pl.when(step == at)
            def _():
                for one in plan[(at, position)]:
                    one()

    def load(ref, m, slot, which):
        return pltpu.make_async_copy(ref.at[m], wide_ref.at[slot, which], load_sem.at[slot, which])

    @pl.when(step == 0)
    def _():
        bring_tok = pltpu.make_async_copy(
            tokens_ref.at[pl.ds(place.z * rows, rows), :], tok_ref, load_sem.at[0, 0]
        )
        bring_past = pltpu.make_async_copy(past_ref, past_vmem, load_sem.at[0, 1])
        bring_tok.start()
        bring_past.start()
        greet(place)
        meta_ref[...] = meta_rows(
            pos_ref[...], counts_ref, place.s * items, PLANE * items, past_ref.shape[2]
        )
        bring_past.wait()
        sampled_ref[...] = pick_samples(past_vmem[...], meta_ref[...], items)
        for part in flat:
            part.first()
        room_ref[...] = small_rows(
            stack_ref[...].astype(F32),
            b_qv_ref[...].astype(F32),
            b_up_ref[...].astype(F32),
            place.s,
            width,
            head,
        )
        for i in range(3):
            attn_ref[:, i * local : (i + 1) * local] = w_qkv_ref[i]
        row, lane = iotas((w_out_ref.shape[1], w_out_ref.shape[1]))
        unit = (row == lane).astype(F32).astype(BF)
        attn_ref[:, 3 * local :] = dot_nt(unit, w_out_ref[...]).astype(BF)
        bring_tok.wait()
        acc_ref[...] = jnp.zeros_like(acc_ref)
        clear_moments(inv_ref, mom_ref)

    transfers(0, 0)

    meta, samples = flat

    @pl.when(step == 1)
    def _():
        for kind in (2, 3):
            meta.part(kind, 0)()
        samples.part(2, 0)()
        meta.own.wait()
        meta.close(0)

    transfers(1, 0)

    @pl.when(step == 1)
    def _():
        def owner(s, carry):
            rows = owner_basis(all_meta_ref[0, pl.ds(s * 8, 8), :], items)
            basis_ref[s] = rows
            inv_ref[...] += dot_tn(rows, rows, HIGHEST)
            return carry

        lax.fori_loop(0, PLANE, owner, 0)
        samples.part(3, 0)()
        samples.own.wait()
        samples.close(0)

    transfers(1, 1)

    @pl.when(step == 1)
    def _():
        def owner(s, carry):
            count = sampled_ref.shape[0]
            rows = all_sampled_ref[0, pl.ds(s * count, count), :]
            mom_ref[...] += dot_tn(basis_ref[s], rows.astype(F32), HIGHEST)
            return carry

        lax.fori_loop(0, PLANE, owner, 0)

    transfers(1, 2)

    inverse_end = 2 + NB // PIVOTS

    @pl.when((step >= 2) & (step < inverse_end))
    def _():
        invert_step(inv_ref)

    for at in range(2, inverse_end):
        transfers(at, 0)

    @pl.when(step == inverse_end)
    def _():
        coef_part_ref[...] = coefficients(inv_ref, mom_ref).astype(BF)
        line.first()

    transfers(inverse_end, 0)

    @pl.when(step == inverse_end)
    def _():
        room.own.wait()
        for m in range(LINE):
            room.close(m)
            total = all_room_ref[m, 0:16, :].astype(F32)
            for s in range(1, PLANE):
                total = total + all_room_ref[m, s * 16 : (s + 1) * 16, :].astype(F32)
            vec_ref[m] = total
        gain, bias = vec_ref[0, 0:1, :], vec_ref[0, 1:2, :]
        normed, _ = norm_parts(tok_ref[...].astype(F32))
        hm_ref[NB:, :] = (normed * gain + bias).astype(BF)
        hmt_ref[:, NB:] = hm_ref[NB:, :].T
        line.step(1)

    transfers(inverse_end, 1)

    @pl.when(step == inverse_end)
    def _():
        attn.own.wait()
        attn.close(0)
        load(wa_ref, 0, 0, 0).start()
        line.step(2)

    transfers(inverse_end, 2)

    @pl.when(step == inverse_end)
    def _():
        line.step(3)
        line.own.wait()
        gain, bias = vec_ref[0, 0:1, :], vec_ref[0, 1:2, :]
        for m in range(LINE):
            coef_ref[:, m * local : (m + 1) * local] = all_coef_ref[m]
        normed, _ = norm_parts(coef_ref[...].astype(F32))
        hm_ref[0:NB, :] = (normed * gain + bias).astype(BF)
        hmt_ref[:, 0:NB] = hm_ref[0:NB, :].T

    @pl.when((step >= attn_at) & (step < mlp_at))
    def _():
        m = step - attn_at
        slot = lax.rem(m, 2)
        load(wa_ref, m, slot, 0).wait()

        @pl.when(m < LINE - 1)
        def _():
            attn.close(m + 1)
            load(wa_ref, m + 1, 1 - slot, 0).start()

        weights = wide_ref[slot, 0]
        projected = project(hm_ref[...], weights, vec_ref[m, 6:7, :], local)
        query = projected[NB:, :local]
        keys = projected[:, local : 2 * local]
        values = projected[:, 2 * local :]
        query_ref[0] = query
        key_ref[0] = keys
        val_ref[0] = values

        def store(h, lines, columns, probs):
            prob_ref[0, h, lines, columns] = probs

        def between(h):
            for at in range(attn_at, mlp_at):
                transfers(at, h)

        attended = attend(query, keys, values, head, store, between)
        att_ref[0] = attended
        acc_ref[...] += dot_nt(attended.T, wide_ref[slot, 0, :, 3 * local :])

    transfers(mlp_at, 0)

    @pl.when(step == mlp_at)
    def _():
        for part in (up, down):
            part.own.wait()
            part.close(0)
        load(wu_ref, 0, 0, 0).start()
        load(wd_ref, 0, 0, 1).start()
        residual = tok_ref[...].astype(F32) + acc_ref[...] + vec_ref[0, 4:5, :]
        res_ref[...] = residual
        normed, _ = norm_parts(residual)
        h2_ref[...] = (normed * vec_ref[0, 2:3, :] + vec_ref[0, 3:4, :]).astype(BF)
        h2t_ref[...] = h2_ref[...].T
        acc_ref[...] = jnp.zeros_like(acc_ref)

    @pl.when(step >= mlp_at)
    def _():
        m = step - mlp_at
        slot = lax.rem(m, 2)
        load(wu_ref, m, slot, 0).wait()
        load(wd_ref, m, slot, 1).wait()

        @pl.when(m < LINE - 1)
        def _():
            up.close(m + 1)
            down.close(m + 1)
            load(wu_ref, m + 1, 1 - slot, 0).start()
            load(wd_ref, m + 1, 1 - slot, 1).start()

        pre = dot(h2_ref[...], wide_ref[slot, 0]) + vec_ref[m, 7:8, :]
        act, slope = gelu_parts(pre)
        act_ref[0] = act
        slope_ref[0] = slope.astype(BF)
        acc_ref[...] += dot_nt(act, wide_ref[slot, 1])

    @pl.when(step == last)
    def _():
        out_ref[...] = (res_ref[...] + acc_ref[...] + vec_ref[0, 5:6, :]).astype(BF)
        for part in flat + wide:
            part.settle()
        line.finish_sends()


SOLVE_STEPS = 3 + NB // PIVOTS


FORWARD_PLAN = (
    (
        (0, 0),
        ((0, 0, 0),),
    ),
    (
        (1, 0),
        ((1, 0, 0), (0, 1, 1), (0, 1, -1),),
    ),
    (
        (1, 1),
        ((0, 1, -2), (0, 1, 2), (1, 1, -1), (1, 1, 1),),
    ),
    (
        (1, 2),
        ((0, 1, -3), (0, 1, 3), (3, 0, 0),),
    ),
    (
        (2, 0),
        ((1, 1, 2), (1, 1, -2),),
    ),
    (
        (4, 0),
        ((0, 2, -3), (0, 2, 3), (1, 2, 0), (0, 2, -1), (0, 2, 1),),
    ),
    (
        (5, 0),
        ((0, 2, 0), (0, 2, -2), (0, 2, 2), (1, 1, -3), (1, 1, 3), (2, 0, 0),),
    ),
    (
        (7, 0),
        ((1, 2, -2), (1, 2, 2), (1, 2, 1), (1, 2, -1),),
    ),
    (
        (8, 0),
        ((3, 1, 1), (3, 1, -1),),
    ),
    (
        (9, 0),
        ((0, 3, 3), (0, 3, -3),),
    ),
    (
        (10, 0),
        ((0, 3, 1), (0, 3, -1), (1, 2, 3), (1, 2, -3), (0, 3, 0), (0, 3, 2), (0, 3, -2), (3, 1, -2), (3, 1, 2),),
    ),
    (
        (10, 1),
        ((3, 1, 3), (3, 1, -3), (1, 3, 0), (1, 3, 1), (1, 3, -2), (1, 3, 3), (1, 3, -1), (1, 3, 2), (1, 3, -3),),
    ),
    (
        (10, 2),
        ((2, 1, -1), (2, 1, 1),),
    ),
    (
        (11, 0),
        ((2, 1, -2), (2, 1, 2),),
    ),
    (
        (11, 1),
        ((2, 1, 3), (2, 1, -3), (3, 2, 0),),
    ),
    (
        (12, 0),
        ((2, 2, 1), (2, 2, -1), (2, 2, 0),),
    ),
    (
        (12, 1),
        ((2, 2, -3), (2, 2, 3), (3, 2, -2), (3, 2, 2),),
    ),
    (
        (13, 0),
        ((3, 2, -1), (3, 2, 1), (2, 2, 2), (2, 2, -2),),
    ),
    (
        (13, 1),
        ((2, 3, -1), (2, 3, 1), (3, 2, 3), (3, 2, -3), (2, 3, 0),),
    ),
    (
        (13, 2),
        ((3, 3, 0), (2, 3, 3), (2, 3, -3),),
    ),
    (
        (14, 1),
        ((3, 3, 1), (3, 3, -1), (3, 3, 2), (3, 3, -2), (2, 3, -2), (2, 3, 2), (3, 3, 3), (3, 3, -3),),
    ),
)


def forward_pass(tokens, past, positions, counts, stack, b_qv, b_up, w_qkv, w_out, up, down, head):
    width = tokens.shape[1]
    rows = tokens.shape[0] // LINE
    items = past.shape[0]
    local = width // LINE
    hidden = up.shape[1]
    heads = local // head
    keyed = NB + rows
    slots = positions.shape[1]
    samples = items * slots
    part = up.shape[0]
    attn_at = SOLVE_STEPS
    mlp_at = attn_at + LINE
    first = lambda i: jnp.clip(i - attn_at, 0, LINE - 1)
    second = lambda i: jnp.clip(i - mlp_at, 0, LINE - 1)
    whole = lambda shape: pl.BlockSpec(shape, lambda i: (0,) * len(shape))
    anywhere = pl.BlockSpec(memory_space=pl.ANY)
    vmem = pl.BlockSpec(memory_space=pltpu.VMEM)
    dma = pltpu.SemaphoreType.DMA
    shape = jax.ShapeDtypeStruct
    return pl.pallas_call(
        functools.partial(forward_kernel, items=items, head=head),
        grid=(mlp_at + LINE,),
        in_specs=[anywhere, anywhere, vmem, pl.BlockSpec(memory_space=pltpu.SMEM)]
        + [vmem] * 5
        + [anywhere, anywhere],
        out_specs=[
            anywhere,
            anywhere,
            anywhere,
            whole((rows, width)),
            whole((rows, width)),
            whole((width, keyed)),
            whole((width, rows)),
            pl.BlockSpec((1, heads, keyed, rows), lambda i: (first(i), 0, 0, 0)),
            pl.BlockSpec((1, keyed, local), lambda i: (first(i), 0, 0)),
            pl.BlockSpec((1, keyed, local), lambda i: (first(i), 0, 0)),
            pl.BlockSpec((1, rows, local), lambda i: (first(i), 0, 0)),
            pl.BlockSpec((1, local, rows), lambda i: (first(i), 0, 0)),
            pl.BlockSpec((1, rows, hidden), lambda i: (second(i), 0, 0)),
            pl.BlockSpec((1, rows, hidden), lambda i: (second(i), 0, 0)),
            whole((LINE, 16, width)),
            whole((NB, NB)),
            whole((NB, width)),
            whole((8, slots)),
        ],
        out_shape=[
            shape((LINE, width, width), BF),
            shape((LINE, width, hidden), BF),
            shape((LINE, width, hidden), BF),
            shape((rows, width), BF),
            shape((rows, width), F32),
            shape((width, keyed), BF),
            shape((width, rows), BF),
            shape((LINE, heads, keyed, rows), BF),
            shape((LINE, keyed, local), BF),
            shape((LINE, keyed, local), BF),
            shape((LINE, rows, local), BF),
            shape((LINE, local, rows), BF),
            shape((LINE, rows, hidden), BF),
            shape((LINE, rows, hidden), BF),
            shape((LINE, 16, width), F32),
            shape((NB, NB), F32),
            shape((NB, width), BF),
            shape((8, slots), F32),
        ],
        scratch_shapes=[
            pltpu.VMEM((keyed, width), BF),
            pltpu.VMEM((rows, width), BF),
            pltpu.VMEM((16, width), BF),
            pltpu.VMEM((part, width), BF),
            pltpu.VMEM((rows, width), BF),
            pltpu.VMEM((rows, width), F32),
            pltpu.VMEM((NB, local), F32),
            pltpu.VMEM((samples, local), BF),
            pltpu.VMEM((1, PLANE * samples, local), BF),
            pltpu.VMEM((PLANE, samples, NB), F32),
            pltpu.VMEM((1, PLANE * 8, slots), F32),
            pltpu.VMEM((LINE, PLANE * 16, width), BF),
            pltpu.VMEM((NB, local), BF),
            pltpu.VMEM((LINE, NB, local), BF),
            pltpu.VMEM((2, 2, width, width), BF),
            pltpu.VMEM(past.shape, BF),
            dma((2, 5, 4)),
            dma((2, PLANE)),
            dma((2,)),
            dma((4, 5, LINE * 4)),
            dma((4, LINE * PLANE)),
            dma((4,)),
            dma((2, LINE)),
            dma((LINE,)),
            dma(()),
            dma((2, 2)),
        ],
        compiler_params=pltpu.CompilerParams(
            collective_id=1, has_side_effects=True, vmem_limit_bytes=BIG_VMEM
        ),
        name="forward_pass",
    )(tokens, past, positions, counts, stack, b_qv, b_up, w_qkv, w_out, up, down)


def plain_forward_kernel(
    tok_ref,
    coef_ref,
    vec_ref,
    wa_ref,
    wu_ref,
    wd_ref,
    out_ref,
    res_ref,
    hm_ref,
    h2_ref,
    prob_ref,
    key_ref,
    val_ref,
    query_ref,
    att_ref,
    act_ref,
    slope_ref,
    acc_ref,
    *,
    groups,
    head,
):
    step = pl.program_id(0)
    rows, width = tok_ref.shape
    local = query_ref.shape[2]

    @pl.when(step == 0)
    def _():
        gain, bias = vec_ref[0, 0:1, :], vec_ref[0, 1:2, :]
        normed, _ = norm_parts(coef_ref[...].astype(F32))
        hm_ref[0:NB, :] = (normed * gain + bias).astype(BF)
        normed, _ = norm_parts(tok_ref[...].astype(F32))
        hm_ref[NB:, :] = (normed * gain + bias).astype(BF)
        acc_ref[...] = jnp.zeros_like(acc_ref)

    @pl.when(step < groups)
    def _():
        weights = wa_ref[0]
        projected = project(hm_ref[...], weights, vec_ref[step, 6:7, :], local)
        query = projected[NB:, :local]
        keys = projected[:, local : 2 * local]
        values = projected[:, 2 * local :]
        query_ref[0] = query
        key_ref[0] = keys
        val_ref[0] = values

        def store(h, lines, columns, probs):
            prob_ref[0, h, lines, columns] = probs

        attended = attend(query, keys, values, head, store, lambda h: None)
        att_ref[0] = attended
        acc_ref[...] += dot_nt(attended.T, weights[:, 3 * local :])

    @pl.when(step == groups)
    def _():
        residual = tok_ref[...].astype(F32) + acc_ref[...] + vec_ref[0, 4:5, :]
        res_ref[...] = residual
        normed, _ = norm_parts(residual)
        h2_ref[...] = (normed * vec_ref[0, 2:3, :] + vec_ref[0, 3:4, :]).astype(BF)
        acc_ref[...] = jnp.zeros_like(acc_ref)

    @pl.when(step >= groups)
    def _():
        pre = dot(h2_ref[...], wu_ref[0]) + vec_ref[step - groups, 7:8, :]
        act, slope = gelu_parts(pre)
        act_ref[0] = act
        slope_ref[0] = slope.astype(BF)
        acc_ref[...] += dot_nt(act, wd_ref[0])

    @pl.when(step == 2 * groups - 1)
    def _():
        out_ref[...] = (res_ref[...] + acc_ref[...] + vec_ref[0, 5:6, :]).astype(BF)


def plain_forward(tok, coef, vec, wide, head):
    rows, width = tok.shape
    groups = wide[0].shape[0]
    local = width // groups
    hidden = wide[1].shape[2]
    heads = local // head
    keyed = NB + rows
    first = lambda i: jnp.minimum(i, groups - 1)
    second = lambda i: jnp.maximum(i - groups, 0)
    whole = lambda shape: pl.BlockSpec(shape, lambda i: (0,) * len(shape))
    shape = jax.ShapeDtypeStruct
    return pl.pallas_call(
        functools.partial(plain_forward_kernel, groups=groups, head=head),
        grid=(2 * groups,),
        in_specs=[
            whole((rows, width)),
            whole((NB, width)),
            whole((groups, 16, width)),
            pl.BlockSpec((1, width, width), lambda i: (first(i), 0, 0)),
            pl.BlockSpec((1, width, hidden), lambda i: (second(i), 0, 0)),
            pl.BlockSpec((1, width, hidden), lambda i: (second(i), 0, 0)),
        ],
        out_specs=[
            whole((rows, width)),
            whole((rows, width)),
            whole((keyed, width)),
            whole((rows, width)),
            pl.BlockSpec((1, heads, keyed, rows), lambda i: (first(i), 0, 0, 0)),
            pl.BlockSpec((1, keyed, local), lambda i: (first(i), 0, 0)),
            pl.BlockSpec((1, keyed, local), lambda i: (first(i), 0, 0)),
            pl.BlockSpec((1, rows, local), lambda i: (first(i), 0, 0)),
            pl.BlockSpec((1, local, rows), lambda i: (first(i), 0, 0)),
            pl.BlockSpec((1, rows, hidden), lambda i: (second(i), 0, 0)),
            pl.BlockSpec((1, rows, hidden), lambda i: (second(i), 0, 0)),
        ],
        out_shape=[
            shape((rows, width), BF),
            shape((rows, width), F32),
            shape((keyed, width), BF),
            shape((rows, width), BF),
            shape((groups, heads, keyed, rows), BF),
            shape((groups, keyed, local), BF),
            shape((groups, keyed, local), BF),
            shape((groups, rows, local), BF),
            shape((groups, local, rows), BF),
            shape((groups, rows, hidden), BF),
            shape((groups, rows, hidden), BF),
        ],
        scratch_shapes=[pltpu.VMEM((rows, width), F32)],
        compiler_params=pltpu.CompilerParams(vmem_limit_bytes=BIG_VMEM),
        name="plain_forward",
    )(tok, coef, vec, *wide)


def attend_back(g_att, att_t, keys, values, query, probs_of, head, between):
    rows, local = g_att.shape
    half = rows // 2
    low = NB + rows - half
    g_att_t = g_att.T
    product = g_att_t.astype(F32) * att_t.astype(F32)
    key_t = keys.T
    scale = 1.0 / math.sqrt(head)
    line = lax.broadcasted_iota(jnp.int32, (local, rows), 0)
    lane = lax.broadcasted_iota(jnp.int32, (rows, local), 1)
    key_grad = [jnp.zeros((low, local), F32), jnp.zeros((half, local), F32)]
    val_grad = [jnp.zeros((low, local), F32), jnp.zeros((half, local), F32)]
    query_grads = []
    for h in range(local // head):
        own_t = (line >= h * head) & (line < (h + 1) * head)
        own = (lane >= h * head) & (lane < (h + 1) * head)
        grad_t = jnp.where(own_t, g_att_t, BF(0.0))
        grad_h = jnp.where(own, g_att, BF(0.0))
        query_h = jnp.where(own, query, BF(0.0))
        inner = jnp.sum(product[h * head : (h + 1) * head, :], axis=0, keepdims=True)
        key_h = key_t[h * head : (h + 1) * head, :]
        parts = []
        for b in range(2):
            span = NB + (b + 1) * half
            cols = slice(b * half, (b + 1) * half)
            probs = probs_of(h, slice(0, span), cols)
            dprob = dot(values[:span, :], grad_t[:, cols])
            dscore = (probs.astype(F32) * (dprob - inner[:, cols])).astype(BF)
            parts.append(dot(key_h[:, :span], dscore))
            val_part = dot(probs, grad_h[cols, :])
            key_part = dot(dscore, query_h[cols, :])
            val_grad[0] = val_grad[0] + val_part[:low, :]
            key_grad[0] = key_grad[0] + key_part[:low, :]
            if b == 1:
                val_grad[1] = val_grad[1] + val_part[low:, :]
                key_grad[1] = key_grad[1] + key_part[low:, :]
        query_grads.append(jnp.concatenate(parts, axis=1))
        between(h)
    query_grad = (jnp.concatenate(query_grads, axis=0) * scale).astype(BF).T
    key_grad = jnp.concatenate(key_grad, axis=0) * scale
    return query_grad, key_grad, jnp.concatenate(val_grad, axis=0)


def backward_kernel(
    tokens_ref,
    cots_ref,
    fwd_out_ref,
    res_ref,
    wa_ref,
    wu_ref,
    wd_ref,
    vec_ref,
    hmt_ref,
    h2t_ref,
    coef_ref,
    inv_ref,
    meta_ref,
    prob_ref,
    key_ref,
    val_ref,
    query_ref,
    att_ref,
    act_ref,
    slope_ref,
    outs_ref,
    tgs_ref,
    past_ref,
    vectors_ref,
    bias_ref,
    bias_up_ref,
    qkv_out_ref,
    wo_out_ref,
    up_out_ref,
    down_out_ref,
    *scratch,
    head,
):
    (
        tok_ref,
        cot_ref,
        cott_ref,
        gres_ref,
        acc_ref,
        proj_ref,
        gv_ref,
        ggv_ref,
        gmem_ref,
        wide_ref,
        side_ref,
        attn_ref,
        mlp_ref,
        gv_mem_ref,
        side_out_ref,
        attn_out_ref,
        mlp_out_ref,
    ) = scratch[:17]
    buffers = scratch[17:32]
    block_sems, sems, lsend, lrecv, lown, gsend, grecv, gown, load_sem = scratch[32:]
    step = pl.program_id(0)
    rows, width = tok_ref.shape
    local = query_ref.shape[2]
    items = past_ref.shape[0]
    place = Place()
    side, attn, mlp = [
        kind(place, grads, out, buffers[i::3], (block_sems.at[i], sems.at[i]))
        for i, (kind, grads, out) in enumerate(
            (
                (DirectCollect, side_ref, side_out_ref),
                (Collect, attn_ref, attn_out_ref),
                (Collect, mlp_ref, mlp_out_ref),
            )
        )
    ]
    outs, tgs = [
        [
            Line(
                place,
                src.at[pl.ds(h * (rows // count), rows // count), :],
                dst.at[:, pl.ds(h * (rows // count), rows // count), :],
                lsend.at[first + h],
                lrecv.at[first + h],
                lown.at[first + h],
            )
            for h in range(count)
        ]
        for src, dst, first, count in (
            (fwd_out_ref, outs_ref, 0, OUT_PIECES),
            (cot_ref, tgs_ref, OUT_PIECES, GRAD_PIECES),
        )
    ]
    mem = DirectSpread(place, side_out_ref.at[0, 0:8, :], gmem_ref, gsend, grecv, gown)
    mine = pl.ds(place.z * rows, rows)

    def load(ref, m, slot, which):
        return pltpu.make_async_copy(ref.at[m], wide_ref.at[slot, which], load_sem.at[slot, which])

    def bring(i, src, dst):
        return pltpu.make_async_copy(src, dst, load_sem.at[2, i])

    bring_cot = bring(0, cots_ref.at[mine, :], cot_ref)
    bring_tok = bring(1, tokens_ref.at[mine, :], tok_ref)
    bring_res = pltpu.make_async_copy(res_ref, gres_ref, load_sem.at[3, 0])

    def past():
        mem.own.wait()
        for m in range(LINE):
            mem.close(m)
        gmem = jnp.concatenate([gmem_ref[m] for m in range(LINE)], axis=0)
        give_past(gmem, coef_ref, vec_ref, inv_ref, meta_ref, past_ref, gv_mem_ref)
        own = side_out_ref[0, 8:16, :]
        own = jnp.concatenate([own[0:2] + gv_mem_ref[0:2, :], own[2:8]], axis=0)
        vectors, biases, bias_up = small_pieces(
            own, place.s, vectors_ref.shape[1], bias_ref.shape[2], head, bias_ref.shape[0]
        )
        vectors_ref[...] = vectors
        for h, bias in enumerate(biases):
            bias_ref[h] = bias
        bias_up_ref[...] = bias_up

    def give_attn():
        attn.result()
        for i in range(3):
            qkv_out_ref[i] = attn_out_ref[0, :, i * local : (i + 1) * local]
        row, lane = iotas((attn_out_ref.shape[1], attn_out_ref.shape[1]))
        unit = (row == lane).astype(F32)
        wo_out_ref[...] = dot_tn(attn_out_ref[0, :, 3 * local :], unit, HIGHEST)

    def give_mlp():
        mlp.result()
        up_out_ref[...] = mlp_out_ref[0]
        down_out_ref[...] = mlp_out_ref[1]

    def move(what, kind, i):
        if what == 1 and kind == 4:
            return [give_attn]
        if what == 2 and kind == 4:
            return [give_mlp]
        if what < 3:
            return [(side, attn, mlp)[what].part(kind, i)]
        if what == 3:
            return mem.steps(kind) if kind else [mem.first]
        if what == 4:
            return [past]
        line = (outs + tgs)[what - 5]
        return [functools.partial(line.step, i) if kind else line.first]

    plan = [[one for what in moves for one in move(*what)] for moves in BACKWARD_PLAN]

    def transfers(slot, condition=None):
        def go():
            for one in plan[slot]:
                one()

        if plan[slot]:
            when((condition,), go)

    @pl.when(step == 0)
    def _():
        bring_cot.start()
        bring_tok.start()
        bring_res.start()
        load(wu_ref, 0, 0, 0).start()
        load(wd_ref, 0, 0, 1).start()
        greet(place, whole_line=True)
        for line in outs:
            line.first()
        acc_ref[...] = jnp.zeros_like(acc_ref)
        gv_ref[...] = jnp.zeros_like(gv_ref)
        bring_cot.wait()
        bring_tok.wait()
        bring_res.wait()
        cott_ref[...] = cot_ref[...].T

    @pl.when(step < LINE)
    def _():
        m = step
        slot = lax.rem(m, 2)
        load(wu_ref, m, slot, 0).wait()
        load(wd_ref, m, slot, 1).wait()

        @pl.when(m < LINE - 1)
        def _():
            load(wu_ref, m + 1, 1 - slot, 0).start()
            load(wd_ref, m + 1, 1 - slot, 1).start()

        @pl.when(m == LINE - 1)
        def _():
            load(wa_ref, 0, 0, 0).start()

        upstream = cot_ref[...]
        grad = (dot(upstream, wide_ref[slot, 1]) * slope_ref[0].astype(F32)).astype(BF)
        mlp_ref[m, 1] = dot(cott_ref[...], act_ref[0]).astype(BF)
        mlp_ref[m, 0] = dot(h2t_ref[...], grad).astype(BF)
        mlp.begin(m)
        for at in range(LINE):
            transfers(at, step == at)
        ggv_ref[m, 1:2, :] = col_sum(grad.astype(F32))
        acc_ref[NB:, :] += dot_nt(grad, wide_ref[slot, 0])

    @pl.when(step == LINE)
    def _():
        transfers(LINE)
        upstream = cot_ref[...].astype(F32)
        normed, inverse = norm_parts(gres_ref[...])
        grad = acc_ref[NB:, :]
        g_res = upstream + norm_back(grad, normed, inverse, vec_ref[0, 2:3, :])
        gres_ref[...] = g_res
        g_attn = g_res.astype(BF)
        gv_ref[2:3, :] = col_sum(grad * normed)
        gv_ref[3:4, :] = col_sum(grad)
        gv_ref[4:5, :] = col_sum(g_attn.astype(F32))
        gv_ref[5:6, :] = col_sum(upstream)
        cott_ref[...] = g_attn.T
        acc_ref[...] = jnp.zeros_like(acc_ref)
        proj_ref[0:NB, :] = jnp.zeros((NB, proj_ref.shape[1]), BF)
        transfers(LINE + 1)

    @pl.when(step >= LINE)
    def _():
        m = step - LINE
        slot = lax.rem(m, 2)
        load(wa_ref, m, slot, 0).wait()

        @pl.when(m < LINE - 1)
        def _():
            load(wa_ref, m + 1, 1 - slot, 0).start()

        def between(h):
            for at in range(LINE):
                transfers(LINE + 2 + 4 * at + h, m == at)

        def probs_of(h, lines, columns):
            return prob_ref[0, h, lines, columns]

        g_attn = gres_ref[...].astype(BF)
        g_att = dot(g_attn, wide_ref[slot, 0, :, 3 * local :]).astype(BF)
        att_t = att_ref[0]
        query_grad, key_grad, val_grad = attend_back(
            g_att, att_t, key_ref[0], val_ref[0], query_ref[0], probs_of, head, between
        )
        proj_ref[NB:, 0:local] = query_grad
        proj_ref[:, local : 2 * local] = key_grad.astype(BF)
        proj_ref[:, 2 * local :] = val_grad.astype(BF)
        proj = proj_ref[...]
        ggv_ref[m, 0:1, 0 : 3 * local] = col_sum(proj.astype(F32))
        ggv_ref[m, 0:1, 3 * local :] = jnp.zeros((1, width - 3 * local), F32)
        attn_ref[m, 0, :, 0 : 3 * local] = dot(hmt_ref[...], proj).astype(BF)
        attn_ref[m, 0, :, 3 * local :] = dot_nt(cott_ref[...], att_t).astype(BF)
        attn.begin(m)
        acc_ref[...] += dot_nt(proj, wide_ref[slot, 0, :, : 3 * local])
        between(3)

    @pl.when(step == 2 * LINE - 1)
    def _():
        grad = acc_ref[NB:, :]
        normed, inverse = norm_parts(tok_ref[...].astype(F32))
        back = norm_back(grad, normed, inverse, vec_ref[0, 0:1, :])
        cot_ref[...] = (gres_ref[...] + back).astype(BF)
        tgs[0].first()
        gv_ref[0:1, :] = col_sum(grad * normed)
        gv_ref[1:2, :] = col_sum(grad)
        transfers(5 * LINE + 2)
        for m in range(LINE):
            below = jnp.concatenate([gv_ref[0:6, :], ggv_ref[m, 0:2, :]], axis=0)
            for s in range(PLANE):
                top = (m * PLANE + s) * 8
                side_ref[m, 0, s * 16 : s * 16 + 8, :] = acc_ref[top : top + 8, :]
                side_ref[m, 0, s * 16 + 8 : (s + 1) * 16, :] = below
            side.begin(m)
        transfers(5 * LINE + 3)
        mem.settle()
        for part in (side, attn, mlp):
            part.settle()
        for line in outs + tgs:
            line.finish()


OUT_PIECES, GRAD_PIECES = 2, 4

BACKWARD_PLAN = (
    (),
    (),
    (),
    (),
    ((5, 1, 1),),
    (),
    ((2, 0, 1),),
    ((6, 1, 1),),
    (),
    ((2, 0, 0),),
    ((2, 1, 0),),
    (),
    ((2, 0, 3),),
    ((5, 1, 2),),
    (),
    ((2, 2, 0),),
    ((1, 0, 1),),
    ((2, 0, 2), (6, 1, 2),),
    (),
    (),
    ((1, 0, 0),),
    (),
    ((8, 0, 0), (1, 0, 3), (1, 0, 2), (9, 0, 0), (10, 0, 0),),
    ((0, 0, 0), (0, 0, 1), (0, 0, 2), (0, 0, 3), (0, 1, 2), (1, 1, 2), (0, 1, 3), (1, 2, 2), (0, 2, 3), (0, 1, 1), (0, 2, 1), (0, 2, 2), (0, 1, 0), (0, 2, 0), (8, 1, 1), (1, 1, 1), (1, 2, 1), (0, 3, 1), (1, 1, 0), (1, 2, 0), (2, 1, 1), (2, 2, 1), (0, 3, 3), (0, 3, 2), (2, 1, 3), (2, 2, 3), (0, 3, 0), (2, 1, 2), (2, 2, 2), (7, 1, 1), (0, 4, 0), (3, 0, 0), (6, 1, 3), (10, 1, 1), (9, 1, 1), (5, 1, 3), (8, 1, 2), (1, 1, 3), (1, 2, 3), (2, 3, 0), (1, 3, 2), (3, 1, 0), (10, 1, 2), (1, 3, 0), (2, 3, 1), (7, 1, 2), (9, 1, 2), (2, 3, 3), (3, 2, 0), (3, 3, 0), (1, 3, 3), (2, 3, 2), (1, 3, 1), (4, 0, 0), (7, 1, 3), (8, 1, 3), (9, 1, 3), (10, 1, 3), (2, 4, 0), (1, 4, 0),),
)


def backward_pass(tokens, cots, out, meta, vec, inverse, coef, saved, wide, items, past_shape, head):
    res, hmt, h2t, prob, keys, vals, query, att, act, slope = saved
    rows, width = out.shape
    local = width // LINE
    hidden = wide[1].shape[2]
    heads = local // head
    keyed = NB + rows
    first = lambda i: jnp.minimum(i, LINE - 1)
    second = lambda i: jnp.maximum(i - LINE, 0)
    anywhere = pl.BlockSpec(memory_space=pl.ANY)
    vmem = pl.BlockSpec(memory_space=pltpu.VMEM)
    dma = pltpu.SemaphoreType.DMA
    shape = jax.ShapeDtypeStruct
    part = width // PLANE
    blocks = ((1, 16, width), (1, part, width), (2, part, width))
    kinds = (F32, BF, BF)
    pieces = OUT_PIECES + GRAD_PIECES
    return pl.pallas_call(
        functools.partial(backward_kernel, head=head),
        grid=(2 * LINE,),
        in_specs=[anywhere] * 7
        + [vmem] * 6
        + [
            pl.BlockSpec((1, heads, keyed, rows), lambda i: (second(i), 0, 0, 0)),
            pl.BlockSpec((1, keyed, local), lambda i: (second(i), 0, 0)),
            pl.BlockSpec((1, keyed, local), lambda i: (second(i), 0, 0)),
            pl.BlockSpec((1, rows, local), lambda i: (second(i), 0, 0)),
            pl.BlockSpec((1, local, rows), lambda i: (second(i), 0, 0)),
            pl.BlockSpec((1, rows, hidden), lambda i: (first(i), 0, 0)),
            pl.BlockSpec((1, rows, hidden), lambda i: (first(i), 0, 0)),
        ],
        out_specs=[anywhere, anywhere] + [vmem] * 8,
        out_shape=[
            shape((LINE, rows, width), BF),
            shape((LINE, rows, width), BF),
            shape(past_shape, F32),
            shape((8, part), F32),
            shape((local // head, 2, head // PLANE), F32),
            shape((head // PLANE, hidden // head), F32),
            shape((3, part, local), F32),
            shape((local, part), F32),
            shape((part, hidden), F32),
            shape((part, hidden), F32),
        ],
        scratch_shapes=[
            pltpu.VMEM((rows, width), BF),
            pltpu.VMEM((rows, width), BF),
            pltpu.VMEM((width, rows), BF),
            pltpu.VMEM((rows, width), F32),
            pltpu.VMEM((keyed, width), F32),
            pltpu.VMEM((keyed, 3 * local), BF),
            pltpu.VMEM((8, width), F32),
            pltpu.VMEM((LINE, 8, hidden), F32),
            pltpu.VMEM((LINE, PLANE * 8, width), F32),
            pltpu.VMEM((2, 2, width, width), BF),
        ]
        + [pltpu.VMEM((LINE, b[0], PLANE * b[1], b[2]), t) for b, t in zip(blocks, kinds)]
        + [pltpu.VMEM((8, width), F32)]
        + [pltpu.VMEM(b, F32) for b in blocks]
        + [pltpu.VMEM(lead + b, t) for lead in BUFFERS for b, t in zip(blocks, kinds)]
        + [
            dma((3, 2, 4, LINE)),
            dma((3, 9, LINE)),
            dma((pieces, 2, LINE)),
            dma((pieces, LINE)),
            dma((pieces,)),
            dma((5, LINE * 4)),
            dma((LINE * PLANE,)),
            dma(()),
            dma((4, 2)),
        ],
        compiler_params=pltpu.CompilerParams(
            collective_id=2, has_side_effects=True, vmem_limit_bytes=MAX_VMEM
        ),
        name="backward_pass",
    )(
        tokens,
        cots,
        out,
        res,
        *wide,
        vec,
        hmt,
        h2t,
        coef,
        inverse,
        meta,
        prob,
        keys,
        vals,
        query,
        att,
        act,
        slope,
    )


def plain_backward_kernel(
    tok_ref,
    cot_ref,
    res_ref,
    vec_ref,
    hm_ref,
    h2_ref,
    prob_ref,
    key_ref,
    val_ref,
    query_ref,
    att_ref,
    act_ref,
    slope_ref,
    wa_ref,
    wu_ref,
    wd_ref,
    tg_ref,
    gmem_ref,
    gup_ref,
    gdown_ref,
    gatt_ref,
    gv_ref,
    ggv_ref,
    acc_ref,
    hmt_ref,
    h2t_ref,
    cott_ref,
    gres_ref,
    proj_ref,
    *,
    groups,
    head,
):
    step = pl.program_id(0)
    rows, width = tok_ref.shape
    local = query_ref.shape[2]

    @pl.when(step == 0)
    def _():
        acc_ref[...] = jnp.zeros_like(acc_ref)
        h2t_ref[...] = h2_ref[...].T
        cott_ref[...] = cot_ref[...].T
        gv_ref[...] = jnp.zeros_like(gv_ref)

    @pl.when(step < groups)
    def _():
        upstream = cot_ref[...]
        grad = (dot(upstream, wd_ref[0]) * slope_ref[0].astype(F32)).astype(BF)
        gdown_ref[0] = dot(cott_ref[...], act_ref[0]).astype(BF)
        gup_ref[0] = dot(h2t_ref[...], grad).astype(BF)
        ggv_ref[0] = jnp.zeros_like(ggv_ref[0])
        ggv_ref[0, 0:1, :] = col_sum(grad.astype(F32))
        acc_ref[NB:, :] += dot_nt(grad, wu_ref[0])

    @pl.when(step == groups)
    def _():
        upstream = cot_ref[...].astype(F32)
        normed, inverse = norm_parts(res_ref[...])
        grad = acc_ref[NB:, :]
        g_res = upstream + norm_back(grad, normed, inverse, vec_ref[2:3, :])
        gres_ref[...] = g_res
        g_attn = g_res.astype(BF)
        gv_ref[2:3, :] = col_sum(grad * normed)
        gv_ref[3:4, :] = col_sum(grad)
        gv_ref[4:5, :] = col_sum(g_attn.astype(F32))
        gv_ref[5:6, :] = col_sum(upstream)
        cott_ref[...] = g_attn.T
        hmt_ref[...] = hm_ref[...].T
        acc_ref[...] = jnp.zeros_like(acc_ref)
        proj_ref[0:NB, :] = jnp.zeros((NB, proj_ref.shape[1]), BF)

    @pl.when(step >= groups)
    def _():
        weights = wa_ref[0]
        g_attn = gres_ref[...].astype(BF)
        g_att = dot(g_attn, weights[:, 3 * local :]).astype(BF)
        att_t = att_ref[0]
        query_grad, key_grad, val_grad = attend_back(
            g_att,
            att_t,
            key_ref[0],
            val_ref[0],
            query_ref[0],
            lambda h, lines, columns: prob_ref[0, h, lines, columns],
            head,
            lambda h: None,
        )
        key_grad, val_grad = key_grad.astype(BF), val_grad.astype(BF)
        proj_ref[NB:, 0:local] = query_grad
        proj_ref[:, local : 2 * local] = key_grad
        proj_ref[:, 2 * local :] = val_grad
        proj = proj_ref[...]
        ggv_ref[0] = jnp.zeros_like(ggv_ref[0])
        ggv_ref[0, 0:1, 0 : 3 * local] = col_sum(proj.astype(F32))
        gatt_ref[0, :, 0 : 3 * local] = dot(hmt_ref[...], proj).astype(BF)
        gatt_ref[0, :, 3 * local :] = dot_nt(cott_ref[...], att_t).astype(BF)
        acc_ref[...] += dot_nt(proj, weights[:, : 3 * local])

    @pl.when(step == 2 * groups - 1)
    def _():
        gmem_ref[...] = acc_ref[0:NB, :]
        grad = acc_ref[NB:, :]
        normed, inverse = norm_parts(tok_ref[...].astype(F32))
        part = norm_back(grad, normed, inverse, vec_ref[0:1, :])
        tg_ref[...] = (gres_ref[...] + part).astype(BF)
        gv_ref[0:1, :] = col_sum(grad * normed)
        gv_ref[1:2, :] = col_sum(grad)


def plain_backward(tok, cot, vec, saved, wide, head):
    res, hm, h2, prob, keys, vals, query, att, act, slope = saved
    rows, width = tok.shape
    groups = wide[0].shape[0]
    local = width // groups
    hidden = wide[1].shape[2]
    heads = local // head
    keyed = NB + rows
    first = lambda i: jnp.minimum(i, groups - 1)
    second = lambda i: jnp.maximum(i - groups, 0)
    whole = lambda shape: pl.BlockSpec(shape, lambda i: (0,) * len(shape))
    return pl.pallas_call(
        functools.partial(plain_backward_kernel, groups=groups, head=head),
        grid=(2 * groups,),
        in_specs=[
            whole((rows, width)),
            whole((rows, width)),
            whole((rows, width)),
            whole((16, width)),
            whole((keyed, width)),
            whole((rows, width)),
            pl.BlockSpec((1, heads, keyed, rows), lambda i: (second(i), 0, 0, 0)),
            pl.BlockSpec((1, keyed, local), lambda i: (second(i), 0, 0)),
            pl.BlockSpec((1, keyed, local), lambda i: (second(i), 0, 0)),
            pl.BlockSpec((1, rows, local), lambda i: (second(i), 0, 0)),
            pl.BlockSpec((1, local, rows), lambda i: (second(i), 0, 0)),
            pl.BlockSpec((1, rows, hidden), lambda i: (first(i), 0, 0)),
            pl.BlockSpec((1, rows, hidden), lambda i: (first(i), 0, 0)),
            pl.BlockSpec((1, width, width), lambda i: (second(i), 0, 0)),
            pl.BlockSpec((1, width, hidden), lambda i: (first(i), 0, 0)),
            pl.BlockSpec((1, width, hidden), lambda i: (first(i), 0, 0)),
        ],
        out_specs=[
            whole((rows, width)),
            whole((NB, width)),
            pl.BlockSpec((1, width, hidden), lambda i: (first(i), 0, 0)),
            pl.BlockSpec((1, width, hidden), lambda i: (first(i), 0, 0)),
            pl.BlockSpec((1, width, width), lambda i: (second(i), 0, 0)),
            whole((8, width)),
            pl.BlockSpec((1, 8, hidden), lambda i: (i, 0, 0)),
        ],
        out_shape=[
            jax.ShapeDtypeStruct((rows, width), BF),
            jax.ShapeDtypeStruct((NB, width), F32),
            jax.ShapeDtypeStruct((groups, width, hidden), BF),
            jax.ShapeDtypeStruct((groups, width, hidden), BF),
            jax.ShapeDtypeStruct((groups, width, width), BF),
            jax.ShapeDtypeStruct((8, width), F32),
            jax.ShapeDtypeStruct((2 * groups, 8, hidden), F32),
        ],
        scratch_shapes=[
            pltpu.VMEM((keyed, width), F32),
            pltpu.VMEM((width, keyed), BF),
            pltpu.VMEM((width, rows), BF),
            pltpu.VMEM((width, rows), BF),
            pltpu.VMEM((rows, width), F32),
            pltpu.VMEM((keyed, 3 * local), BF),
        ],
        compiler_params=pltpu.CompilerParams(vmem_limit_bytes=BIG_VMEM),
        name="plain_backward",
    )(
        tok, cot, res, vec, hm, h2, prob, keys, vals, query, att, act, slope, *wide
    )


def local(
    tokens,
    cotangent,
    past_state,
    positions,
    counts,
    ln1_gain,
    ln1_bias,
    w_qkv,
    b_qv,
    w_out,
    b_out,
    ln2_gain,
    ln2_bias,
    w_up,
    b_up,
    w_down,
    b_down,
):
    seq, mp = lax.axis_size("seq"), lax.axis_size("mp")
    seq_index, mp_index = lax.axis_index("seq"), lax.axis_index("mp")
    item_count, seg_len, local_width = past_state.shape
    slots = positions.shape[1]
    total = item_count * seq
    width = tokens.shape[1]
    part = width // seq
    heads_local, piece = b_qv.shape[1], b_qv.shape[2]
    head = piece * seq
    hidden = w_up.shape[1]
    rows = tokens.shape[0] // mp
    direct = seq == PLANE and mp == LINE and part % 16 == 0 and hidden == width

    past_t = past_state.transpose(0, 2, 1)

    vectors = jnp.stack([ln1_gain, ln1_bias, ln2_gain, ln2_bias, b_out, b_down])
    if direct:
        results = forward_pass(
            tokens,
            past_t,
            positions,
            counts,
            vectors,
            b_qv.transpose(1, 0, 2),
            b_up.T,
            w_qkv,
            w_out,
            w_up,
            w_down.T,
            head,
        )
        wide, forward, (vec, inverse, coef, meta) = results[:3], results[3:14], results[14:]
        block_out, block_grad, past_grad, vec_own, bias, bias_up, qkv_grad, out_grad, *mlp = (
            backward_pass(
                tokens,
                cotangent,
                forward[0],
                meta,
                vec,
                inverse,
                coef,
                forward[1:],
                wide,
                item_count,
                past_t.shape,
                head,
            )
        )
        block_out = block_out.reshape(mp * rows, width)
        block_grad = block_grad.reshape(mp * rows, width)
        qv, up, (up_grad, down_grad) = bias.transpose(1, 0, 2), bias_up.T, mlp
    else:
        items = (seq_index * item_count + jnp.arange(item_count)).astype(F32)
        spots = positions.astype(F32)
        places = (items[:, None] + (spots + 0.5) / seg_len) / total
        used = (jnp.arange(slots)[None, :] < counts[:, None]).astype(F32)
        meta = jnp.concatenate([places, used, spots, jnp.zeros((8 - 3 * item_count, slots), F32)])

        here = (jnp.arange(seq) == seq_index).astype(BF)
        vectors = (vectors[:, None, :] * here[None, :, None]).reshape(6, width)
        bias_qv = (b_qv[:, :, None, :] * here[None, None, :, None]).reshape(2, local_width)
        bias_qv = jnp.concatenate([bias_qv, jnp.zeros((2, local_width), BF)], axis=1)
        bias_up = (b_up[:, None, :] * here[None, :, None]).reshape(1, hidden)
        room = jnp.concatenate(
            [vectors, bias_qv.reshape(1, width), bias_up, jnp.zeros((8, width), BF)]
        )
        attn = jnp.concatenate([w_qkv[0], w_qkv[1], w_qkv[2], w_out.T], axis=1)
        sampled = sample_rows(past_t, meta)
        all_sampled = lax.all_gather(sampled, "seq", axis=0)
        all_meta = lax.all_gather(meta, "seq", axis=0)
        coef_part, inverse = solve_memory(all_sampled, all_meta, item_count)
        coef = lax.all_gather(coef_part, "mp", axis=0).transpose(1, 0, 2).reshape(NB, width)
        wide = [
            lax.all_gather(lax.all_gather(shard, "seq", axis=0, tiled=True), "mp", axis=0)
            for shard in (attn, w_up, w_down.T)
        ]
        vec = lax.psum(room.astype(F32), "seq")
        vec = lax.all_gather(vec, "mp", axis=0)
        tok = lax.dynamic_slice_in_dim(tokens, mp_index * rows, rows, 0)
        cot = lax.dynamic_slice_in_dim(cotangent, mp_index * rows, rows, 0)
        forward = plain_forward(tok, coef, vec, wide, head)
        block_out = lax.all_gather(forward[0], "mp", axis=0, tiled=True)
        tok_grad, gmem, g_up, g_down, g_attn, gv, ggv = plain_backward(
            tok, cot, vec[0], forward[1:], wide, head
        )
        tail = jnp.concatenate(
            [jnp.broadcast_to(gv[None, :6], (mp, 6, width)), ggv[mp:, :1], ggv[:mp, :1]], axis=1
        )
        block_grad = lax.all_gather(tok_grad, "mp", axis=0, tiled=True)
        gmem, tail = lax.psum((gmem, tail), ("seq", "mp"))
        own = lax.dynamic_index_in_dim(tail, mp_index, 0, keepdims=False)
        attn, up_grad, down_grad = (
            lax.psum_scatter(
                lax.psum_scatter(g, "mp", scatter_dimension=0, tiled=False),
                "seq",
                scatter_dimension=0,
                tiled=True,
            ).astype(F32)
            for g in (g_attn, g_up, g_down)
        )
        past_grad, gv_mem = past_grads(
            gmem, coef, vec, inverse, meta, item_count, seg_len, local_width
        )
        own = own + jnp.concatenate([gv_mem[:2], jnp.zeros((6, width), F32)])
        vec_own = lax.dynamic_slice_in_dim(own[:6], seq_index * part, part, 1)
        qv = jnp.stack([own[6, :local_width], own[6, 2 * local_width : 3 * local_width]])
        qv = qv.reshape(2, heads_local, head)
        qv = lax.dynamic_slice_in_dim(qv, seq_index * piece, piece, 2)
        up = lax.dynamic_slice_in_dim(own[7].reshape(-1, head), seq_index * piece, piece, 1)
        qkv_grad = jnp.stack([attn[:, i * local_width : (i + 1) * local_width] for i in range(3)])
        out_grad = attn[:, 3 * local_width :].T
    return (
        block_out,
        block_grad,
        past_grad.transpose(0, 2, 1),
        vec_own[0],
        vec_own[1],
        qkv_grad,
        qv,
        out_grad,
        vec_own[4],
        vec_own[2],
        vec_own[3],
        up_grad,
        up,
        down_grad.T,
        vec_own[5],
    )


def solution(mesh):
    row = P("seq", None)
    placed = (
        row,
        row,
        P("seq", None, "mp"),
        row,
        P("seq"),
        P("seq"),
        P("seq"),
        P(None, "seq", "mp"),
        P(None, "mp", "seq"),
        P("mp", "seq"),
        P("seq"),
        P("seq"),
        P("seq"),
        P("seq", "mp"),
        P("mp", "seq"),
        P("mp", "seq"),
        P("seq"),
    )
    return jax.shard_map(
        local,
        mesh=mesh,
        in_specs=placed,
        out_specs=(row, row, placed[2]) + placed[5:],
        check_vma=False,
    )
```

profile of v0, /device:TPU:0, one launch (start us, length us, event | category | flops | bytes accessed | tf_op | source)
XLA Modules:
  0.0 242.4 jit_solution(12063970758878142332)
XLA Ops:
  0.6 1.3 stack.27.stack_ref
  2.0 100.4 %forward_pass.1 = (bf16[4,768,768]{2,1,0:T(8,128)(2,1)}, bf16[4,768,768]{2,1,0:T(8,128)(2,1)}, bf16[4,768,768]{2,1,0:T(8,128)(2,1)}, bf16[512,768]{1,0:T(8,128)(...) custom-call(bf16[2048,768]{1,0:T(8,128)(2,1)} %tokens_ref.3, ...), custom_call_target="tpu_custom_call" | custom-call | tf_op jit(solution)/shard_map/forward_pass/pallas_call | solution.py:1220
  102.4 128.1 %backward_pass.1 = (bf16[4,512,768]{2,1,0:T(8,128)(2,1)}, bf16[4,512,768]{2,1,0:T(8,128)(2,1)}, f32[2,192,512]{2,1,0:T(8,128)}, f32[8,96]{1,0:T(8,128)}, f32[3,2...) custom-call(bf16[2048,768]{1,0:T(8,128)(2,1)} %tokens_ref.3, ...), custom_call_target="tpu_custom_call" | custom-call | tf_op jit(solution)/shard_map/backward_pass/pallas_call | solution.py:1794
  230.5 1.4 slice_bitcast_fusion
  231.9 0.0 copy-start
  231.9 3.9 %copy.41 = bf16[2048,768]{1,0:T(8,128)(2,1)} copy(bf16[2048,768]{1,0:T(8,128)(2,1)} %bitcast.29) | data formatting | bytes 6291456
  235.8 0.0 copy-done
  235.8 0.0 copy-start.1
  235.8 0.0 copy-start.4
  235.8 0.0 copy-start.7
  235.8 0.0 copy-start.5
  235.8 0.0 copy-start.3
  235.8 0.0 copy-start.6
  235.8 0.0 copy-start.2
  235.8 1.7 copy.42
  237.5 0.0 copy-done.1
  237.5 0.9 copy.43
  238.4 0.0 copy-done.4
  238.4 0.7 copy.44
  239.1 0.0 copy-done.7
  239.1 0.6 copy.45
  239.7 0.0 copy-done.5
  239.7 0.6 copy.46
  240.3 0.0 copy-done.3
  240.3 0.7 copy.47
  241.1 0.0 copy-done.6
  241.1 0.6 copy.48
  241.7 0.0 copy-done.2
  241.7 0.7 copy.49
Async XLA Ops:
  231.9 3.9 %copy-start = (bf16[4,512,768]{2,1,0:T(8,128)(2,1)S(1)}, bf16[4,512,768]{2,1,0:T(8,128)(2,1)}, u32[]{:S(2)}) copy-start(bf16[4,512,768]{2,1,0:T(8,128)(2,1)} %get-tuple-element.62) | copy-start | bytes 9437188
  235.8 1.7 copy-start.1
  235.8 2.6 %copy-start.4 = (f32[3,96,192]{2,1,0:T(8,128)S(1)}, f32[3,96,192]{2,1,0:T(8,128)}, u32[]{:S(2)}) copy-start(f32[3,96,192]{2,1,0:T(8,128)} %get-tuple-element.97) | copy-start | bytes 663556
  235.8 3.3 %copy-start.7 = (f32[3,2,8]{2,1,0:T(2,128)S(1)}, f32[3,2,8]{2,1,0:T(2,128)}, u32[]{:S(2)}) copy-start(f32[3,2,8]{2,1,0:T(2,128)} %get-tuple-element.66) | copy-start | bytes 580
  235.8 3.9 %copy-start.5 = (f32[192,96]{1,0:T(8,128)S(1)}, f32[192,96]{1,0:T(8,128)}, u32[]{:S(2)}) copy-start(f32[192,96]{1,0:T(8,128)} %get-tuple-element.99) | copy-start | bytes 221188
  235.8 4.5 %copy-start.3 = (f32[96,768]{1,0:T(8,128)S(1)}, f32[96,768]{1,0:T(8,128)}, u32[]{:S(2)}) copy-start(f32[96,768]{1,0:T(8,128)} %get-tuple-element.103) | copy-start | bytes 884740
  235.8 5.2 %copy-start.6 = (f32[8,12]{1,0:T(8,128)S(1)}, f32[8,12]{1,0:T(8,128)}, u32[]{:S(2)}) copy-start(f32[8,12]{1,0:T(8,128)} %get-tuple-element.69) | copy-start | bytes 1156
  235.8 5.8 %copy-start.2 = (f32[96,768]{1,0:T(8,128)S(1)}, f32[96,768]{1,0:T(8,128)}, u32[]{:S(2)}) copy-start(f32[96,768]{1,0:T(8,128)} %get-tuple-element.70) | copy-start | bytes 884740
where the time goes:
time: 243 us; the launch traced here: 242 us
  Pallas kernels  228 us (94%)
  local copies, waits for them, and re-layouts  13.2 us (5%)
    pallas_call x1, Pallas kernels, backward_pass(): pl.pallas_call(functools.partial(backward_kernel, head=head), grid=(2 * L...  128 us
    pallas_call x1, Pallas kernels, forward_pass(): pl.pallas_call(functools.partial(forward_kernel, items=items, head=head),...  100 us
    unnamed x25, local copies, waits for them, and re-layouts  10.4 us

commit v1 on v0

--- a/solution.py
+++ b/solution.py
@@ -2046,6 +2046,31 @@
     )
 
 
+def hand_over_kernel(*refs):
+    half = len(refs) // 2
+    for src, dst in zip(refs[:2], refs[half : half + 2]):
+        dst[...] = src[0]
+
+    @pl.when(pl.program_id(0) == 0)
+    def _():
+        for src, dst in zip(refs[2:half], refs[half + 2 :]):
+            dst[...] = src[...]
+
+
+def hand_over(rows, others):
+    count, n, width = rows[0].shape
+    whole = [pl.BlockSpec(a.shape, lambda i, r=a.ndim: (0,) * r) for a in others]
+    return pl.pallas_call(
+        hand_over_kernel,
+        grid=(count,),
+        in_specs=[pl.BlockSpec((1, n, width), lambda i: (i, 0, 0))] * len(rows) + whole,
+        out_specs=[pl.BlockSpec((n, width), lambda i: (i, 0))] * len(rows) + whole,
+        out_shape=[jax.ShapeDtypeStruct((count * n, width), a.dtype) for a in rows]
+        + [jax.ShapeDtypeStruct(a.shape, a.dtype) for a in others],
+        name="hand_over",
+    )(*rows, *others)
+
+
 def local(
     tokens,
     cotangent,
@@ -2097,24 +2122,24 @@
             head,
         )
         wide, forward, (vec, inverse, coef, meta) = results[:3], results[3:14], results[14:]
-        block_out, block_grad, past_grad, vec_own, bias, bias_up, qkv_grad, out_grad, *mlp = (
-            backward_pass(
-                tokens,
-                cotangent,
-                forward[0],
-                meta,
-                vec,
-                inverse,
-                coef,
-                forward[1:],
-                wide,
-                item_count,
-                past_t.shape,
-                head,
-            )
-        )
-        block_out = block_out.reshape(mp * rows, width)
-        block_grad = block_grad.reshape(mp * rows, width)
+        block_out, block_grad, *others = backward_pass(
+            tokens,
+            cotangent,
+            forward[0],
+            meta,
+            vec,
+            inverse,
+            coef,
+            forward[1:],
+            wide,
+            item_count,
+            past_t.shape,
+            head,
+        )
+        vec_own = others.pop(1)
+        (block_out, block_grad, past_grad, bias, bias_up, qkv_grad, out_grad, *mlp) = hand_over(
+            [block_out, block_grad], others
+        )
         qv, up, (up_grad, down_grad) = bias.transpose(1, 0, 2), bias_up.T, mlp
     else:
         items = (seq_index * item_count + jnp.arange(item_count)).astype(F32)

time: 243 us -> 238 us (0.979)
  local copies, waits for them, and re-layouts: 13.2 us -> 1.87 us
  Pallas kernels: 228 us -> 236 us
    unnamed x25 -> x2, local copies, waits for them, and re-layouts: 10.4 us -> 0.01 us
    pallas_call x0 -> x1, Pallas kernels: none -> 7.08 us  [hand_over(): pl.pallas_call(hand_over_kernel, grid=(count,), in_specs=[pl.BlockSpec((1...]
where the time goes in v1:
time: 238 us
  Pallas kernels  236 us (99%)
    pallas_call x1, Pallas kernels, backward_pass(): pl.pallas_call(functools.partial(backward_kernel, head=head), grid=(2 * L...  128 us
    pallas_call x1, Pallas kernels, forward_pass(): pl.pallas_call(functools.partial(forward_kernel, items=items, head=head),...  100 us
    pallas_call x1, Pallas kernels, hand_over(): pl.pallas_call(hand_over_kernel, grid=(count,), in_specs=[pl.BlockSpec((1...  7.08 us

profile of v1, /device:TPU:0, one launch (start us, length us, event | category | flops | bytes accessed | tf_op | source)
XLA Modules:
  0.0 238.2 jit_solution(6561677268094398802)
XLA Ops:
  0.6 1.3 stack.27.stack_ref
  2.0 100.4 %forward_pass.1 = (bf16[4,768,768]{2,1,0:T(8,128)(2,1)}, bf16[4,768,768]{2,1,0:T(8,128)(2,1)}, bf16[4,768,768]{2,1,0:T(8,128)(2,1)}, bf16[512,768]{1,0:T(8,128)(...) custom-call(bf16[2048,768]{1,0:T(8,128)(2,1)} %tokens_ref.3, ...), custom_call_target="tpu_custom_call" | custom-call | tf_op jit(solution)/shard_map/forward_pass/pallas_call | solution.py:1220
  102.4 128.1 %backward_pass.1 = (bf16[4,512,768]{2,1,0:T(8,128)(2,1)}, bf16[4,512,768]{2,1,0:T(8,128)(2,1)}, f32[2,192,512]{2,1,0:T(8,128)}, f32[8,96]{1,0:T(8,128)}, f32[3,2...) custom-call(bf16[2048,768]{1,0:T(8,128)(2,1)} %tokens_ref.3, ...), custom_call_target="tpu_custom_call" | custom-call | tf_op jit(solution)/shard_map/backward_pass/pallas_call | solution.py:1794
  230.5 0.0 copy-start
  230.5 7.1 %hand_over.1 = (bf16[2048,768]{1,0:T(8,128)(2,1)}, bf16[2048,768]{1,0:T(8,128)(2,1)}, f32[2,192,512]{2,1,0:T(8,128)}, f32[3,2,8]{2,1,0:T(2,128)}, f32[8,12]{1,0:...) custom-call(bf16[4,512,768]{2,1,0:T(8,128)(2,1)} %get-tuple-element.70.refs_0_, ...), custom_call_target="tpu_custom_call" | custom-call | tf_op jit(solution)/shard_map/hand_over/pallas_call | solution.py:2063
  237.6 0.0 copy-done
  237.6 0.5 slice_bitcast_fusion
Async XLA Ops:
  230.5 7.1 %copy-start = (f32[8,96]{1,0:T(8,128)S(1)}, f32[8,96]{1,0:T(8,128)}, u32[]{:S(2)}) copy-start(f32[8,96]{1,0:T(8,128)} %get-tuple-element.82) | copy-start | bytes 9220

commit v2 on v1

--- a/solution.py
+++ b/solution.py
@@ -2046,29 +2046,50 @@
     )
 
 
-def hand_over_kernel(*refs):
-    half = len(refs) // 2
-    for src, dst in zip(refs[:2], refs[half : half + 2]):
-        dst[...] = src[0]
-
-    @pl.when(pl.program_id(0) == 0)
-    def _():
-        for src, dst in zip(refs[2:half], refs[half + 2 :]):
-            dst[...] = src[...]
+def hand_over_kernel(*refs, count, rows):
+    srcs, dsts, held = refs[:count], refs[count : 2 * count], refs[2 * count : 3 * count]
+    sems = refs[3 * count]
+    moves = []
+    for i, (src, dst, mid) in enumerate(zip(srcs, dsts, held)):
+        if i < rows:
+            n = src.shape[1]
+            for m in range(LINE):
+                moves.append((src.at[m], mid.at[m], dst.at[pl.ds(m * n, n), :]))
+        else:
+            moves.append((src, mid, dst))
+    copies = [
+        (
+            pltpu.make_async_copy(src, mid, sems.at[0, i]),
+            pltpu.make_async_copy(mid, dst, sems.at[1, i]),
+        )
+        for i, (src, mid, dst) in enumerate(moves)
+    ]
+    for bring, _ in copies:
+        bring.start()
+    for bring, give in copies:
+        bring.wait()
+        give.start()
+    for _, give in copies:
+        give.wait()
 
 
 def hand_over(rows, others):
-    count, n, width = rows[0].shape
-    whole = [pl.BlockSpec(a.shape, lambda i, r=a.ndim: (0,) * r) for a in others]
+    arrays = rows + others
+    anywhere = pl.BlockSpec(memory_space=pl.ANY)
+    moves = len(rows) * LINE + len(others)
     return pl.pallas_call(
-        hand_over_kernel,
-        grid=(count,),
-        in_specs=[pl.BlockSpec((1, n, width), lambda i: (i, 0, 0))] * len(rows) + whole,
-        out_specs=[pl.BlockSpec((n, width), lambda i: (i, 0))] * len(rows) + whole,
-        out_shape=[jax.ShapeDtypeStruct((count * n, width), a.dtype) for a in rows]
+        functools.partial(hand_over_kernel, count=len(arrays), rows=len(rows)),
+        in_specs=[anywhere] * len(arrays),
+        out_specs=[anywhere] * len(arrays),
+        out_shape=[
+            jax.ShapeDtypeStruct((a.shape[0] * a.shape[1], a.shape[2]), a.dtype) for a in rows
+        ]
         + [jax.ShapeDtypeStruct(a.shape, a.dtype) for a in others],
+        scratch_shapes=[pltpu.VMEM(a.shape, a.dtype) for a in arrays]
+        + [pltpu.SemaphoreType.DMA((2, moves))],
+        compiler_params=pltpu.CompilerParams(vmem_limit_bytes=16 * 1024 * 1024),
         name="hand_over",
-    )(*rows, *others)
+    )(*arrays)
 
 
 def local(

time: 238 us -> 246 us (1.034)
  local copies, waits for them, and re-layouts: 1.87 us -> 11.9 us
  Pallas kernels: 236 us -> 233 us
    unnamed x2 -> x20, local copies, waits for them, and re-layouts: 0.01 us -> 10 us
    pallas_call x1, Pallas kernels: 7.08 us -> 4.26 us  [hand_over(): pl.pallas_call(functools.partial(hand_over_kernel, count=len(arrays), row...]
where the time goes in v2:
time: 246 us; the launch traced here: 245 us
  Pallas kernels  233 us (95%)
  local copies, waits for them, and re-layouts  11.9 us (5%)
    pallas_call x1, Pallas kernels, backward_pass(): pl.pallas_call(functools.partial(backward_kernel, head=head), grid=(2 * L...  128 us
    pallas_call x1, Pallas kernels, forward_pass(): pl.pallas_call(functools.partial(forward_kernel, items=items, head=head),...  100 us
    unnamed x20, local copies, waits for them, and re-layouts  10 us

profile of v2, /device:TPU:0, one launch (start us, length us, event | category | flops | bytes accessed | tf_op | source)
XLA Modules:
  0.0 245.3 jit_solution(9069905696340247234)
XLA Ops:
  0.6 1.3 stack.27.stack_ref
  2.0 100.4 %forward_pass.1 = (bf16[4,768,768]{2,1,0:T(8,128)(2,1)}, bf16[4,768,768]{2,1,0:T(8,128)(2,1)}, bf16[4,768,768]{2,1,0:T(8,128)(2,1)}, bf16[512,768]{1,0:T(8,128)(...) custom-call(bf16[2048,768]{1,0:T(8,128)(2,1)} %tokens_ref.3, ...), custom_call_target="tpu_custom_call" | custom-call | tf_op jit(solution)/shard_map/forward_pass/pallas_call | solution.py:1220
  102.3 128.1 %backward_pass.1 = (bf16[4,512,768]{2,1,0:T(8,128)(2,1)}, bf16[4,512,768]{2,1,0:T(8,128)(2,1)}, f32[2,192,512]{2,1,0:T(8,128)}, f32[8,96]{1,0:T(8,128)}, f32[3,2...) custom-call(bf16[2048,768]{1,0:T(8,128)(2,1)} %tokens_ref.3, ...), custom_call_target="tpu_custom_call" | custom-call | tf_op jit(solution)/shard_map/backward_pass/pallas_call | solution.py:1794
  230.4 0.0 copy-start
  230.4 1.9 copy-done
  232.3 0.0 copy-start.1
  232.3 1.9 copy-done.1
  234.2 0.0 copy-start.2
  234.2 1.1 copy-done.2
  235.4 0.0 copy-start.3
  235.4 1.0 copy-done.3
  236.3 0.0 copy-start.4
  236.3 1.0 copy-done.4
  237.3 0.0 copy-start.5
  237.3 1.0 copy-done.5
  238.2 0.0 copy-start.6
  238.2 0.9 copy-done.6
  239.1 0.0 copy-start.7
  239.1 0.7 copy-done.7
  239.8 0.0 copy-start.8
  239.8 0.7 copy-done.8
  240.5 0.0 copy-start.9
  240.5 4.3 %hand_over.1 = (bf16[2048,768]{1,0:T(8,128)(2,1)}, bf16[2048,768]{1,0:T(8,128)(2,1)}, f32[2,192,512]{2,1,0:T(8,128)}, f32[3,2,8]{2,1,0:T(2,128)}, f32[8,12]{1,0:...) custom-call(bf16[4,512,768]{2,1,0:T(8,128)(2,1)S(1)} %copy-done, ...), custom_call_target="tpu_custom_call" | custom-call | tf_op jit(solution)/shard_map/hand_over/pallas_call | solution.py:2080
  244.7 0.0 copy-done.9
  244.8 0.5 slice_bitcast_fusion
Async XLA Ops:
  230.4 1.9 copy-start
  232.3 1.9 copy-start.1
  234.2 1.1 copy-start.2
  235.4 1.0 copy-start.3
  236.3 1.0 copy-start.4
  237.3 1.0 copy-start.5
  238.2 0.9 copy-start.6
  239.1 0.7 copy-start.7
  239.8 0.7 copy-start.8
  240.5 4.3 %copy-start.9 = (f32[8,96]{1,0:T(8,128)S(1)}, f32[8,96]{1,0:T(8,128)}, u32[]{:S(2)}) copy-start(f32[8,96]{1,0:T(8,128)} %get-tuple-element.82) | copy-start | bytes 9220
